TPU v7x, 256 devices: a whole 4x4x8 slice. The times are simulated.
256 devices in a mesh: dp: 16 (over y, x), tensor: 8 (over z), layers: 2 (over core).
Axes of the slice: x: 4, y: 4, z: 8, core: 2. Of those that a mesh axis runs over, the one named last changes fastest.
Arguments:
- section_input: bfloat16 [2, 2048, 4096], P('layers', 'dp', 'tensor'), may hold values from -24 to 24
- out_cotangent: bfloat16 [2048, 4096], P('dp', 'tensor'), may hold values from -24 to 24
- lift_weight: bfloat16 [2, 2048, 4096], P('layers', None, 'tensor'), may hold values from -0.125 to 0.125
- proj_weight: bfloat16 [2, 4096, 4096], P('layers', None, 'tensor'), may hold values from -0.09375 to 0.09375
- lift_mask: int32 [2, 16, 32], P('layers', None, 'tensor'), may hold values 0 or 1
- proj_mask: int32 [2, 32, 32], P('layers', None, 'tensor'), may hold values 0 or 1
- channel_perm: int32 [2, 4096], P('layers'), may hold values from 0 to 4095, each once within a row
- lift_moment: float32 [2, 2048, 4096], P('layers', 'dp', 'tensor'), may hold values from -3 to 3
- lift_square: float32 [2, 2048, 4096], P('layers', 'dp', 'tensor'), may hold values from 0.25 to 1
- proj_moment: float32 [2, 4096, 4096], P('layers', 'dp', 'tensor'), may hold values from -3 to 3
- proj_square: float32 [2, 4096, 4096], P('layers', 'dp', 'tensor'), may hold values from 0.25 to 1
Outputs:
- input_grad: float32 [2, 2048, 4096], P('layers', 'dp', 'tensor')
- log_det: float32 [2], P('layers')
- lift_first: float32 [2, 2048, 4096], P('layers', 'dp', 'tensor')
- lift_second: float32 [2, 2048, 4096], P('layers', 'dp', 'tensor')
- lift_update: float32 [2, 2048, 4096], P('layers', 'dp', 'tensor')
- proj_first: float32 [2, 4096, 4096], P('layers', 'dp', 'tensor')
- proj_second: float32 [2, 4096, 4096], P('layers', 'dp', 'tensor')
- proj_update: float32 [2, 4096, 4096], P('layers', 'dp', 'tensor')
Inputs may be any that keep to these rules, and one draw needn't show every extreme that they name: `channel_perm`: each row orders all 4096 features once. `lift_mask`: 1 keeps a block of 128 x 128 weights, 0 prunes it. `proj_mask`: 1 keeps a block of 128 x 128 weights, 0 prunes it.
All inputs are finite; a program needn't handle non-finite values.
Results may differ from a plain program's by a relative error of at most 0.008.
Values may be sent and summed in bfloat16 or wider, within the bound.
A program may use at most 128 MiB of HBM per device.

v0:
```python
import functools

import jax
import jax.numpy as jnp
from jax import lax
from jax.sharding import Mesh
from jax.sharding import PartitionSpec as P

BLK = 128
ADAM_STEP = 10
CLIP = 4096
DP = ("dp_0", "dp_1")
DP_TENSOR_LAYERS = ("dp_0", "dp_1", "tensor", "layers")


beta_one = 0.9
beta_two = 0.99
adam_eps = 1e-08


def side_by_side(arrays, axis, dim, along):
    both = jnp.concatenate(arrays, axis=along)
    whole, at, finished = (lax.all_gather(both, axis, axis=dim, tiled=True), 0, [])
    for a in arrays:
        finished.append(lax.slice_in_dim(whole, at, at + a.shape[along], axis=along))
        at += a.shape[along]
    return tuple(finished)


def over_pieces(array, axis):
    return lax.all_gather(array, axis).astype(jnp.float32).sum(0)


def passed_along(block, axis, distance):
    devices = range(lax.axis_size(axis))
    route = [(i - distance, i) for i in devices if i - distance in devices]
    return lax.ppermute(block, axis, route)


def over_axes(array, axes):
    return functools.reduce(lax.psum, axes, array)


def expand_blocks(block_mask):
    blk_rows, blk_cols = block_mask.shape
    widened = jnp.broadcast_to((block_mask > 0)[:, None, :, None], (blk_rows, BLK, blk_cols, BLK))
    return widened.reshape(blk_rows * BLK, blk_cols * BLK)


def contract_rows(left_mat, right_mat):
    return lax.dot_general(
        left_mat, right_mat, (((0,), (0,)), ((), ())), preferred_element_type=jnp.float32
    )


def contract_cols(left_mat, right_mat):
    return lax.dot_general(
        left_mat, right_mat, (((1,), (1,)), ((), ())), preferred_element_type=jnp.float32
    )


def adam_step(gradient, kept, moment, square, factor):
    scaled = gradient * factor
    new_first = jnp.where(kept, beta_one * moment + (1.0 - beta_one) * scaled, moment)
    new_second = jnp.where(kept, beta_two * square + (1.0 - beta_two) * scaled * scaled, square)
    bias_one = 1.0 - beta_one**ADAM_STEP
    bias_two = 1.0 - beta_two**ADAM_STEP
    update = jnp.where(
        kept, new_first / bias_one / (jnp.sqrt(new_second / bias_two) + adam_eps), 0.0
    )
    return (new_first[None], new_second[None], update[None])


def per_device(
    section_input,
    out_cotangent,
    lift_weight,
    proj_weight,
    lift_mask,
    proj_mask,
    channel_perm,
    lift_moment,
    lift_square,
    proj_moment,
    proj_square,
):
    section_idx = lax.axis_index("layers")
    dp_size = lax.axis_size(DP)
    dp_index = lax.axis_index(DP)
    tensor_size = lax.axis_size("tensor")
    tensor_index = lax.axis_index("tensor")
    tokens, gathered_cot = side_by_side((section_input[0], out_cotangent), "tensor", 1, 0)
    channel_order = channel_perm[0]
    feat_width = channel_order.shape[0]
    half_width = feat_width // 2
    tok_rows = tokens.shape[0]
    lift_keep = expand_blocks(lift_mask[0])
    proj_keep = expand_blocks(proj_mask[0])
    lift_eff = jnp.where(lift_keep, lift_weight[0], jnp.zeros((), jnp.bfloat16))
    proj_eff = jnp.where(proj_keep, proj_weight[0], jnp.zeros((), jnp.bfloat16))
    permuted = jnp.take(tokens, channel_order, axis=1)
    cond_side = permuted[:, :half_width]
    moved_side = permuted[:, half_width:].astype(jnp.float32)
    pre_act = jnp.dot(cond_side, lift_eff, preferred_element_type=jnp.float32)
    hidden = jax.nn.silu(pre_act).astype(jnp.bfloat16)
    shared = lax.psum(contract_cols(hidden, proj_eff).astype(jnp.bfloat16), "tensor").astype(
        jnp.float32
    )
    raw_scale = shared[:, :half_width]
    shift_term = shared[:, half_width:]
    scale_term = jax.nn.sigmoid(raw_scale + 2.0)
    keep_part = 1.0 - scale_term
    squash = jax.nn.sigmoid(pre_act)
    silu_slope = squash * (1.0 + pre_act * (1.0 - squash))
    inverse = (
        jnp.zeros((feat_width,), jnp.int32)
        .at[channel_order]
        .set(jnp.arange(feat_width, dtype=jnp.int32))
    )
    own_cols = half_width // tensor_size
    own_raw = lax.dynamic_slice_in_dim(raw_scale, tensor_index * own_cols, own_cols, 1)
    log_part = jnp.sum(jax.nn.log_sigmoid(own_raw + 2.0))

    def backward(grad_out):
        grad_cond = grad_out[:, :half_width]
        grad_moved = grad_out[:, half_width:]
        grad_raw = grad_moved * (moved_side + shift_term) * scale_term * keep_part - keep_part
        grad_shift = grad_moved * scale_term
        grad_st = jnp.concatenate([grad_raw, grad_shift], axis=1).astype(jnp.bfloat16)
        grad_act = jnp.dot(grad_st, proj_eff, preferred_element_type=jnp.float32)
        grad_pre = (grad_act * silu_slope).astype(jnp.bfloat16)
        grad_inputs = grad_cond + over_pieces(
            contract_cols(grad_pre, lift_eff).astype(jnp.bfloat16), "tensor"
        ).astype(jnp.float32)
        grad_mixed = jnp.concatenate([grad_inputs, grad_shift], axis=1)
        return (grad_mixed, grad_st, grad_pre)

    incoming = gathered_cot.astype(jnp.float32)
    early_mixed = backward(incoming)[0]
    early_grad = jnp.take(early_mixed, inverse, axis=1)
    passed = passed_along(early_grad.astype(jnp.bfloat16), "layers", -1)
    arriving = jnp.where(section_idx == 0, passed.astype(jnp.float32), incoming)
    grad_mixed, grad_st, grad_pre = backward(arriving)
    lift_rows = lift_moment.shape[1]
    proj_rows = proj_moment.shape[1]
    cond_cols, st_cols = (
        lax.all_to_all(cond_side, DP, split_axis=1, concat_axis=0, tiled=True),
        lax.all_to_all(grad_st, DP, split_axis=1, concat_axis=0, tiled=True),
    )
    pieces = side_by_side((grad_pre, hidden), DP, 0, 1)
    lift_grad = contract_rows(cond_cols, pieces[0])
    proj_grad = contract_rows(st_cols, pieces[1])
    lift_own = lax.dynamic_slice_in_dim(lift_keep, dp_index * lift_rows, lift_rows, 0)
    proj_own = lax.dynamic_slice_in_dim(proj_keep, dp_index * proj_rows, proj_rows, 0)
    lift_grad = jnp.where(lift_own, lift_grad, 0.0)
    proj_grad = jnp.where(proj_own, proj_grad, 0.0)
    local_sq = jnp.sum(lift_grad * lift_grad) + jnp.sum(proj_grad * proj_grad)
    section_slots = jnp.where(jnp.arange(2) == section_idx, log_part, 0.0)
    log_slots, square_total = (
        over_axes(section_slots, DP_TENSOR_LAYERS),
        over_axes(local_sq, DP_TENSOR_LAYERS),
    )
    log_total = jnp.sum(jnp.where(jnp.arange(2) == section_idx, log_slots, 0.0))
    factor = jnp.minimum(1.0, CLIP / (jnp.sqrt(square_total) + 1e-06))
    lift_out = adam_step(lift_grad, lift_own, lift_moment[0], lift_square[0], factor)
    proj_out = adam_step(proj_grad, proj_own, proj_moment[0], proj_square[0], factor)
    grad_cols = feat_width // tensor_size
    own_inverse = lax.dynamic_slice_in_dim(inverse, tensor_index * grad_cols, grad_cols, 0)
    input_grad = jnp.take(grad_mixed, own_inverse, axis=1)[None]
    log_det = (log_total / (tok_rows * dp_size * half_width)).reshape(1)
    return (
        input_grad,
        log_det,
        lift_out[0],
        lift_out[1],
        lift_out[2],
        proj_out[0],
        proj_out[1],
        proj_out[2],
    )


def solution(mesh):
    finer = Mesh(
        mesh.devices.reshape(4, 4, mesh.shape["tensor"], mesh.shape["layers"]),
        ("dp_0", "dp_1", "tensor", "layers"),
    )
    return jax.shard_map(
        per_device,
        mesh=finer,
        in_specs=(
            P("layers", DP, "tensor"),
            P(DP, "tensor"),
            P("layers", None, "tensor"),
            P("layers", None, "tensor"),
            P("layers", None, "tensor"),
            P("layers", None, "tensor"),
            P("layers", None),
            P("layers", DP, "tensor"),
            P("layers", DP, "tensor"),
            P("layers", DP, "tensor"),
            P("layers", DP, "tensor"),
        ),
        out_specs=(
            P("layers", DP, "tensor"),
            P("layers"),
            P("layers", DP, "tensor"),
            P("layers", DP, "tensor"),
            P("layers", DP, "tensor"),
            P("layers", DP, "tensor"),
            P("layers", DP, "tensor"),
            P("layers", DP, "tensor"),
        ),
        check_vma=False,
    )
```

profile of v0, /device:TPU:1, one launch (start us, length us, event | category | flops | bytes accessed | tf_op | source)
XLA Modules:
  0.0 439.0 jit_solution(12635905943048459885)
XLA Ops:
  7.2 1.7 pad_maximum_fusion.3
  12.0 38.8 %all-gather.7.cloned.1.call-done = bf16[256,4096]{1,0:T(8,128)(2,1)} async-done(((bf16[256,512]{1,0:T(8,128)(2,1)}), bf16[256,4096]{1,0:T(8,128)(2,1)}) %all-gather.7.cloned.1.call-update) | async-done | bytes 2097168 | tf_op jit(solution)/shard_map/all_gather | solution.py:23
  50.8 3.2 slice_convert_fusion
  54.7 12.1 %gather_fusion = bf16[4096,128]{1,0:T(8,128)(2,1)S(1)} fusion(bf16[128,4096]{0,1:T(8,128)(2,1)S(1)} %copy.27, s32[4096]{0:T(1024)S(1)} %broadcast_clamp_fusion), kind=kCustom, calls=%fused_computation | custom fusion | bytes 2113536 | tf_op jit(solution)/shard_map/jit(_take)/gather | solution.py:101
  73.8 2.8 convolution_convert_fusion
  76.7 74.5 %all-reduce.6.cloned.1.call-done = bf16[128,4096]{1,0:T(8,128)(2,1)} async-done(((bf16[128,4096]{1,0:T(8,128)(2,1)}), bf16[128,4096]{1,0:T(8,128)(2,1)}) %all-reduce.6.cloned.1.call-update) | async-done | bytes 1048592 | tf_op jit(solution)/shard_map/psum | solution.py:106
  152.6 2.6 fusion.12
  156.5 6.9 %convolution_convert_fusion.2 = bf16[128,2048]{1,0:T(8,128)(2,1)} fusion(bf16[1,4096,512]{2,1,0:T(8,128)(2,1)} %param.14, bf16[128,2048]{1,0:T(8,128)(2,1)} %slice_multiply_fusion.1, bf16[128,2048]{1,0:T(8,128)(2,1)} %fusion.12, bf16[1,2048,512]{2,1,0:T(8,128)(2,1)} %param.13, f32[128,512]{1,0:T(8,128)} %get-tuple-element.46, ...), kind=kOutput, calls=%fused_computation.11 | convolution fusion | flops 811401216 | bytes 11272192 | tf_op jit(solution)/shard_map/dot_general | solution.py:57
  163.4 15.5 %scatter_custom_fusion = s32[4096]{0:T(1024)S(1)} fusion(s32[4096]{0:T(1024)S(1)} %bitcast.161, s32[4096]{0:T(1024)S(1)} %iota.7, s32[]{:T(128)} %constant.33.clone.1), kind=kCustom, calls=%fused_computation.87 | custom fusion | bytes 16388 | tf_op jit(solution)/shard_map/scatter | solution.py:118
  179.0 41.9 %all-gather.11.cloned.1.call-done = bf16[1024,2048]{1,0:T(8,128)(2,1)} async-done(((bf16[128,2048]{1,0:T(8,128)(2,1)}), bf16[1024,2048]{1,0:T(8,128)(2,1)}) %all-gather.11.cloned.1.call-update) | async-done | bytes 4194320 | tf_op jit(solution)/shard_map/all_gather | solution.py:31
  220.9 3.1 convert_reduce_fusion.1
  226.2 1.6 copy.31
  227.9 15.0 %gather_fusion.1 = bf16[4096,128]{1,0:T(8,128)(2,1)} fusion(bf16[128,4096]{0,1:T(8,128)(2,1)S(1)} %copy.31, s32[4096]{0:T(1024)S(1)} %fusion.33), kind=kCustom, calls=%fused_computation.1 | custom fusion | bytes 2113536 | tf_op jit(solution)/shard_map/jit(_take)/gather | solution.py:140
  245.5 3.7 collective-permute-start
  250.9 1.9 convert_select_fusion
  258.0 1.7 convolution_convert_fusion.1
  260.6 2.4 copy.69
  268.1 6.5 %all-to-all-start.1 = ((bf16[128,16,256]{2,0,1:T(8,128)(2,1)}), bf16[128,16,256]{2,0,1:T(8,128)(2,1)S(1)}, u32[]{:S(2)}, u32[]{:S(2)}) async-start(bf16[128,16,256]{2,0,1:T(8,128)(2,1)} %pad_maximum_fusion.2), calls=%async_computation.1 | async-start | bytes 2097152 | tf_op jit(solution)/shard_map/all_to_all | solution.py:148
  274.7 38.1 %all-gather.13.cloned.1.call-done = bf16[1024,2048]{1,0:T(8,128)(2,1)} async-done(((bf16[128,2048]{1,0:T(8,128)(2,1)}), bf16[1024,2048]{1,0:T(8,128)(2,1)}) %all-gather.13.cloned.1.call-update) | async-done | bytes 4194320 | tf_op jit(solution)/shard_map/all_gather | solution.py:31
  312.8 3.1 convert_reduce_fusion
  317.3 1.8 copy.33
  319.1 2.6 gather_fusion.2
  321.8 6.5 %all-to-all-start = ((bf16[128,16,128]{2,0,1:T(8,128)(2,1)}), bf16[128,16,128]{2,0,1:T(8,128)(2,1)S(1)}, u32[]{:S(2)}, u32[]{:S(2)}) async-start(bf16[128,16,128]{2,0,1:T(8,128)(2,1)} %copy_bitcast_fusion.4), calls=%async_computation | async-start | bytes 1048576 | tf_op jit(solution)/shard_map/all_to_all | solution.py:147
  328.5 46.1 %all-gather.9.cloned.1.call-done = bf16[2048,1024]{1,0:T(8,128)(2,1)} async-done(((bf16[128,1024]{1,0:T(8,128)(2,1)}), bf16[2048,1024]{1,0:T(8,128)(2,1)}) %all-gather.9.cloned.1.call-update) | async-done | bytes 4194320 | tf_op jit(solution)/shard_map/all_gather | solution.py:23
  374.6 3.7 multiply_reduce_fusion
  378.4 2.8 multiply_reduce_fusion.1
  383.4 8.9 %all-reduce.2 = (f32[2]{0:T(128)S(1)}, f32[]{:T(128)}) all-reduce(f32[2]{0:T(128)S(1)} %compare_select_fusion.6, f32[]{:T(128)S(6)} %add.161), channel_id=1, replica_groups=mesh['dp_0'=4,'dp_1'=4,'tensor'=8,'layers'=2] {'dp_0'}, use_global_device_ids=true, to_apply=%region_5.6 | all-reduce | flops 3 | bytes 24 | tf_op jit(solution)/shard_map/psum | solution.py:41
  392.3 7.2 %all-reduce.1 = (f32[2]{0:T(128)S(1)}, f32[]{:T(128)}) all-reduce(f32[2]{0:T(128)S(1)} %get-tuple-element.28, f32[]{:T(128)} %get-tuple-element.29), channel_id=1, replica_groups=mesh['dp_0'=4,'dp_1'=4,'tensor'=8,'layers'=2] {'dp_1'}, use_global_device_ids=true, to_apply=%region_6.7 | all-reduce | flops 3 | bytes 24 | tf_op jit(solution)/shard_map/psum | solution.py:41
  399.5 14.3 %all-reduce = (f32[2]{0:T(128)S(1)}, f32[]{:T(128)}) all-reduce(f32[2]{0:T(128)S(1)} %get-tuple-element.26, f32[]{:T(128)} %get-tuple-element.27), channel_id=1, replica_groups=mesh['dp_0'=4,'dp_1'=4,'tensor'=8,'layers'=2] {'tensor'}, use_global_device_ids=true, to_apply=%region_7.8 | all-reduce | flops 3 | bytes 24 | tf_op jit(solution)/shard_map/psum | solution.py:41
  413.8 11.3 %all-reduce.3 = (f32[2]{0:T(128)S(1)}, f32[]{:T(128)}) all-reduce(f32[2]{0:T(128)S(1)} %get-tuple-element.24, f32[]{:T(128)} %get-tuple-element.25), channel_id=1, replica_groups=mesh['dp_0'=4,'dp_1'=4,'tensor'=8,'layers'=2] {'layers'}, use_global_device_ids=true, to_apply=%region_8.9 | all-reduce | flops 3 | bytes 24 | tf_op jit(solution)/shard_map/psum | solution.py:41
  427.1 2.4 select_bitcast_fusion.1
  429.5 1.9 select_bitcast_fusion.2
  (112 shorter events, 33.2 us)
Async XLA Ops:
  7.2 43.7 %all-gather.7.cloned.1.call-start = ((), (), s32[]{:S(2)}) async-start(), calls=%async_computation.2 | async-start | bytes 2359296 | tf_op jit(solution)/shard_map/all_gather | solution.py:23
  8.9 142.2 %all-reduce.6.cloned.1.call-start = ((), (), s32[]{:S(2)}) async-start(), calls=%async_computation.3 | async-start | bytes 2097152 | tf_op jit(solution)/shard_map/psum | solution.py:106
  67.4 2.4 copy-start.27
  67.6 85.0 %copy-start.7 = (bf16[128,4096]{1,0:T(8,128)(2,1)}, bf16[128,4096]{1,0:T(8,128)(2,1)S(1)}, u32[]{:S(2)}) copy-start(bf16[128,4096]{1,0:T(8,128)(2,1)S(1)} %select_bitcast_fusion) | copy-start | bytes 3145732
  68.2 3.1 copy-start.10
  69.8 4.1 copy-start.25
  76.6 144.3 %all-gather.11.cloned.1.call-start = ((), (), s32[]{:S(2)}) async-start(), calls=%async_computation.5 | async-start | bytes 4718592 | tf_op jit(solution)/shard_map/all_gather | solution.py:31
  152.6 2.6 copy-start
  163.4 149.4 %all-gather.13.cloned.1.call-start = ((), (), s32[]{:S(2)}) async-start(), calls=%async_computation.6 | async-start | bytes 4718592 | tf_op jit(solution)/shard_map/all_gather | solution.py:31
  220.9 3.1 copy-start.1
  245.5 5.4 %collective-permute-start = (bf16[128,4096]{1,0:T(8,128)(2,1)}, bf16[128,4096]{1,0:T(8,128)(2,1)}, u32[]{:S(2)}, u32[]{:S(2)}) collective-permute-start(bf16[128,4096]{1,0:T(8,128)(2,1)} %fusion.14), channel_id=1, source_target_pairs={{1,0},{3,2},{5,4},{7,6},{9,8},{11,10},{13,12},{15,14},{17,16},{19,... | collective-permute-start | bytes 3145736 | tf_op jit(solution)/shard_map/ppermute | solution.py:37
  249.3 3.6 copy-start.8
  250.9 3.7 copy-start.26
  252.9 3.0 copy-start.5
  252.9 3.2 copy-start.29
  254.6 2.9 copy-start.16
  254.6 2.9 copy-start.18
  256.1 1.9 copy-start.28
  258.0 2.6 copy-start.6
  259.7 114.9 %all-gather.9.cloned.1.call-start = ((), (), s32[]{:S(2)}) async-start(), calls=%async_computation.4 | async-start | bytes 4456448 | tf_op jit(solution)/shard_map/all_gather | solution.py:23
  260.5 2.4 copy-start.13
  263.0 2.5 copy-start.9
  264.5 2.5 copy-start.17
  264.5 2.5 copy-start.19
  268.1 53.6 %all-to-all-start.1 = ((bf16[128,16,256]{2,0,1:T(8,128)(2,1)}), bf16[128,16,256]{2,0,1:T(8,128)(2,1)S(1)}, u32[]{:S(2)}, u32[]{:S(2)}) async-start(bf16[128,16,256]{2,0,1:T(8,128)(2,1)} %pad_maximum_fusion.2), calls=%async_computation.1 | async-start | bytes 2097152 | tf_op jit(solution)/shard_map/all_to_all | solution.py:148
  312.8 3.1 copy-start.3
  321.8 56.6 %all-to-all-start = ((bf16[128,16,128]{2,0,1:T(8,128)(2,1)}), bf16[128,16,128]{2,0,1:T(8,128)(2,1)S(1)}, u32[]{:S(2)}, u32[]{:S(2)}) async-start(bf16[128,16,128]{2,0,1:T(8,128)(2,1)} %copy_bitcast_fusion.4), calls=%async_computation | async-start | bytes 1048576 | tf_op jit(solution)/shard_map/all_to_all | solution.py:147
  378.3 48.8 %copy-start.20 = (f32[1,256,512]{2,1,0:T(8,128)S(1)}, f32[1,256,512]{2,1,0:T(8,128)}, u32[]{:S(2)}) copy-start(f32[1,256,512]{2,1,0:T(8,128)} %param.20) | copy-start | bytes 1572868
  378.3 48.8 %copy-start.21 = (f32[1,256,512]{2,1,0:T(8,128)S(1)}, f32[1,256,512]{2,1,0:T(8,128)}, u32[]{:S(2)}) copy-start(f32[1,256,512]{2,1,0:T(8,128)} %param.21) | copy-start | bytes 1572868
  378.3 48.8 %copy-start.22 = (f32[256,512]{1,0:T(8,128)S(1)}, f32[256,512]{1,0:T(8,128)}, u32[]{:S(2)}) copy-start(f32[256,512]{1,0:T(8,128)} %get-tuple-element.50) | copy-start | bytes 1572868
  381.2 48.3 %copy-start.23 = (f32[1,128,512]{2,1,0:T(8,128)S(1)}, f32[1,128,512]{2,1,0:T(8,128)}, u32[]{:S(2)}) copy-start(f32[1,128,512]{2,1,0:T(8,128)} %param.18) | copy-start | bytes 786436
  381.2 48.3 %copy-start.24 = (f32[1,128,512]{2,1,0:T(8,128)S(1)}, f32[1,128,512]{2,1,0:T(8,128)}, u32[]{:S(2)}) copy-start(f32[1,128,512]{2,1,0:T(8,128)} %param.19) | copy-start | bytes 786436
  (6 other events, 8.1 us)
Sparse Core Ops, SparseCore 0:
  10.3 40.4 all-gather.6
  76.7 74.3 all-reduce.5
  163.5 57.4 all-gather.10
  259.9 52.8 all-gather.12
  315.6 58.9 all-gather.8
where the time goes:
time: 440 us; the launch traced here: 439 us
  waiting for transfers between devices  241 us (55%)
  local copies, waits for them, and re-layouts  66.6 us (15%)
  blocking collectives  41.7 us (9%)
  other arithmetic  32.9 us (7%)
  matrix products  20.9 us (5%)
  between operations  18.8 us (4%)
  starting transfers between devices  17 us (4%)
    all_gather x2, waiting for transfers between devices, side_by_side(): lax.all_gather(both, axis, axis=dim, tiled=True)  84.9 us
    all_gather x2, waiting for transfers between devices, over_pieces(): return lax.all_gather(array, axis).astype(jnp.float32).sum(0)  80 us
    psum x1, waiting for transfers between devices, per_device(): lax.psum(contract_cols(hidden, proj_eff).astype(jnp.bfloat16), 'tensor')  74.5 us
    psum x4, blocking collectives, over_axes(): return functools.reduce(lax.psum, axes, array)  41.7 us
    gather x2, local copies, waits for them, and re-layouts, per_device(): early_grad = jnp.take(early_mixed, inverse, axis=1)  16.5 us
    scatter x1, local copies, waits for them, and re-layouts, per_device(): inverse = jnp.zeros((feat_width,), jnp.int32).at[channel_order].set(jnp.a...  15.5 us
    gather x2, local copies, waits for them, and re-layouts, per_device(): permuted = jnp.take(tokens, channel_order, axis=1)  12.7 us
    unnamed x63, local copies, waits for them, and re-layouts  12.1 us
  transfers between devices with their start and end apart: 8, of which 6 were waited for; matrix products, arithmetic and copies ran while one was open for 9% of the time, Pallas kernels for 0%

commit v1 on v0

v1 whole, which is shorter than its diff:
```python
import jax
import jax.numpy as jnp
from jax import lax
from jax.experimental import pallas as pl
from jax.experimental.pallas import tpu as pltpu
from jax.sharding import Mesh
from jax.sharding import PartitionSpec as P

BLK = 128
ADAM_STEP = 10
CLIP = 4096
DP = ("dp_0", "dp_1")
MESH = pl.DeviceIdType.MESH
F32 = jnp.float32
BF16 = jnp.bfloat16

NZ = 8
NR = 4

beta_one = 0.9
beta_two = 0.99
adam_eps = 1e-08


def nn(a, b):
    return jnp.dot(a, b, preferred_element_type=F32)


def nt(a, b):
    return lax.dot_general(a, b, (((1,), (1,)), ((), ())), preferred_element_type=F32)


def tn(a, b):
    return lax.dot_general(a, b, (((0,), (0,)), ((), ())), preferred_element_type=F32)


def al(i, m):
    return pl.multiple_of(i, m)


def remote(src, dst, ssem, rsem, **where):
    return pltpu.make_async_remote_copy(
        src_ref=src, dst_ref=dst, send_sem=ssem, recv_sem=rsem, device_id=where, device_id_type=MESH
    )


def both_ways(d, s, h):
    return s < 3 or d == h


def token_kernel(
    x_ref,
    cot_ref,
    lift_ref,
    proj_ref,
    lmask_ref,
    pmask_ref,
    perm_ref,
    gin_ref,
    logp_ref,
    condc_ref,
    stc_ref,
    hid_ref,
    gp_ref,
    xbuf,
    pc,
    m,
    lift,
    proj,
    acc,
    cond,
    moved,
    slope,
    pre,
    stbuf,
    sbuf,
    rbuf,
    cbuf,
    c0buf,
    gbuf,
    cown,
    ag_s,
    ag_r,
    rs_s,
    rs_r,
    cs,
    cr,
    gs,
    gr,
    hs,
    hr,
    a_s,
    a_r,
    ts,
    tr,
    xs,
    xr,
):
    z = lax.axis_index("tensor")
    y = lax.axis_index("dp_0")
    x = lax.axis_index("dp_1")
    core = lax.axis_index("layers")
    me = y * NR + x
    tok = x_ref.shape[0]
    half = tok // 2
    quart = tok // 4
    w = x_ref.shape[1]
    q = w // 2
    hw = NZ * q

    def rows(h):
        return pl.ds(h * half, half)

    def zr(i):
        return lax.rem(z + NZ + i, NZ)

    zside = (zr(1), zr(-1))

    bar = pltpu.get_barrier_semaphore()
    for i in range(1, NZ):
        pl.semaphore_signal(bar, inc=1, device_id={"tensor": zr(i)}, device_id_type=MESH)
    for oy in range(NR):
        for ox in range(NR):
            if oy or ox:
                pl.semaphore_signal(
                    bar,
                    inc=1,
                    device_id={"dp_0": lax.rem(y + oy, NR), "dp_1": lax.rem(x + ox, NR)},
                    device_id_type=MESH,
                )
    pl.semaphore_signal(bar, inc=1, device_id={"layers": 1 - core}, device_id_type=MESH)
    pl.semaphore_wait(bar, NZ - 1 + NR * NR - 1 + 1)

    def ag_copy(p, buf, own, s, d, h):
        origin = zr(-s) if d == 0 else zr(s)
        src = own.at[rows(h)] if s == 0 else buf.at[origin, rows(h)]
        return remote(src, buf.at[origin, rows(h)], ag_s.at[p, d, s, h], ag_r.at[p, d, s, h], tensor=zside[d])

    def ag_wait(p, buf, s, d, h):
        origin = zr(-1 - s) if d == 0 else zr(1 + s)
        ref = buf.at[origin, rows(h)]
        remote(ref, ref, ag_s.at[p, d, s, h], ag_r.at[p, d, s, h], tensor=zside[d]).wait_recv()

    def ag_start(p, buf, own):
        for d in (0, 1):
            for h in (d, 1 - d):
                ag_copy(p, buf, own, 0, d, h).start()

    def ag_step(p, buf, own, s):
        for k in (0, 1):
            for d in (0, 1):
                h = d if k == 0 else 1 - d
                if both_ways(d, s, h):
                    ag_wait(p, buf, s, d, h)
                    if s < 3 and both_ways(d, s + 1, h):
                        ag_copy(p, buf, own, s + 1, d, h).start()
        return [zr(-1 - s), zr(1 + s)] if s < 3 else [zr(4)]

    def ag_finish(p, buf, own):
        for d in (0, 1):
            for s in range(4):
                for h in (0, 1):
                    if both_ways(d, s, h):
                        ag_copy(p, buf, own, s, d, h).wait_send()

    def rs_copy(p, s, d, h):
        return remote(
            sbuf.at[p, d, s, rows(h)],
            rbuf.at[p, d, s, rows(h)],
            rs_s.at[p, d, s, h],
            rs_r.at[p, d, s, h],
            tensor=zside[d],
        )

    def rs(p, part, tick):
        far = part(zr(4))
        for d in (0, 1):
            sbuf[p, d, 0, rows(d)] = far[d * half : (d + 1) * half].astype(BF16)
            rs_copy(p, 0, d, d).start()
        for s in (1, 2, 3):
            mine = [part(zr(4 - s)), part(zr(s - 4))]
            for k in (0, 1):
                for d in (0, 1):
                    h = (1 - d if s == 1 else d) if k == 0 else (d if s == 1 else 1 - d)
                    own = mine[d][h * half : (h + 1) * half]
                    if s > 1 or h == d:
                        rs_copy(p, s - 1, d, h).wait_recv()
                        own = own + rbuf[p, d, s - 1, rows(h)].astype(F32)
                    sbuf[p, d, s, rows(h)] = own.astype(BF16)
                    rs_copy(p, s, d, h).start()
            tick(s)
        own = part(z)
        for d in (0, 1):
            for h in (0, 1):
                rs_copy(p, 3, d, h).wait_recv()
        return own + rbuf[p, 0, 3].astype(F32) + rbuf[p, 1, 3].astype(F32)

    def rs_finish(p):
        for d in (0, 1):
            for s in range(4):
                for h in (0, 1):
                    if s > 0 or h == d:
                        rs_copy(p, s, d, h).wait_send()

    def along(axis, i):
        if axis == "dp_1":
            return {"dp_1": lax.rem(x + NR + i, NR)}
        return {"dp_0": lax.rem(y + NR + i, NR)}

    def slot(buf, stage, h, off, r):
        axis = ("dp_1", "dp_0")[(h + stage) % 2]
        yy, xx = (y, lax.rem(x + NR + off, NR)) if axis == "dp_1" else (lax.rem(y + NR + off, NR), x)
        if stage == 0:
            return buf.at[yy, xx, r]
        return buf.at[yy, :, r] if axis == "dp_0" else buf.at[:, xx, r]

    def xy_rows(h, t, d):
        if t == 0:
            return rows(h)
        return pl.ds(h * half + d * quart, quart)

    def xy_copy(p, buf, stage, h, t, d):
        axis = ("dp_1", "dp_0")[(h + stage) % 2]
        step = 1 if d == 0 else -1
        src = slot(buf, stage, h, 0 if t == 0 else -step, xy_rows(h, t, d))
        return remote(
            src, src, xs.at[p, stage, h, t, d], xr.at[p, stage, h, t, d], **along(axis, step)
        )

    def xy_wait(p, buf, stage, h, t, d):
        axis = ("dp_1", "dp_0")[(h + stage) % 2]
        step = 1 if d == 0 else -1
        ref = slot(buf, stage, h, -step if t == 0 else -2 * step, xy_rows(h, t, d))
        remote(
            ref, ref, xs.at[p, stage, h, t, d], xr.at[p, stage, h, t, d], **along(axis, step)
        ).wait_recv()

    def xy_tick(p, buf, k):
        stage, t = k // 2, k % 2
        if k:
            ps, pt = (k - 1) // 2, (k - 1) % 2
            for h in (0, 1):
                for d in (0, 1):
                    xy_wait(p, buf, ps, h, pt, d)
        if k < 4:
            for h in (0, 1):
                for d in (0, 1):
                    xy_copy(p, buf, stage, h, t, d).start()

    def xy_finish(p, buf):
        for stage in (0, 1):
            for h in (0, 1):
                for t in (0, 1):
                    for d in (0, 1):
                        xy_copy(p, buf, stage, h, t, d).wait_send()

    ag_start(0, xbuf, x_ref)

    @pl.when(core == 1)
    def _():
        for e in (0, 1):
            dest = lax.rem(2 * z + e, NZ)
            piece = cot_ref.at[:, pl.ds(e * q, q)]
            land = cbuf.at[:, pl.ds(al((z // 4) * q, q), q)]

            @pl.when(dest != z)
            def _():
                remote(piece, land, cs.at[e], cr.at[z // 4], tensor=dest).start()

            @pl.when(dest == z)
            def _():
                cbuf[:, pl.ds(al((z // 4) * q, q), q)] = cot_ref[:, pl.ds(e * q, q)]

    def mask_rows(i, _):
        r = pl.ds(al(i * BLK, BLK), BLK)
        for c in range(w // BLK):
            cc = pl.ds(c * BLK, BLK)
            keep = lmask_ref[i, c].astype(F32)
            lift[r, cc] = (lift_ref[r, cc].astype(F32) * keep).astype(BF16)
        return 0

    def mask_rows_proj(i, _):
        r = pl.ds(al(i * BLK, BLK), BLK)
        for c in range(w // BLK):
            cc = pl.ds(c * BLK, BLK)
            keep = pmask_ref[i, c].astype(F32)
            proj[r, cc] = (proj_ref[r, cc].astype(F32) * keep).astype(BF16)
        return 0

    ca_perm = pl.ds(al(z * q, q), q)
    mv_perm = pl.ds(al(hw + z * q, q), q)

    def hot(base, order):
        at = lax.broadcasted_iota(jnp.int32, (BLK, q), 0) + base
        return jnp.where(at == order, 1.0, 0.0).astype(BF16)

    def build(origin):
        def body(i, _):
            base = origin * w + i * BLK
            r = pl.ds(al(base, BLK), BLK)
            for c in range(hw // q):
                cc = pl.ds(c * q, q)
                pc[r, cc] = hot(base, perm_ref[:, cc])
            m[r, pl.ds(w, q)] = hot(base, perm_ref[:, ca_perm])
            m[r, pl.ds(w + q, q)] = hot(base, perm_ref[:, mv_perm])
            return 0

        lax.fori_loop(0, w // BLK, body, 0)

    def pick(origin, first, src):
        r = pl.ds(al(origin * w, w), w)
        block = src[...]

        def body(c, _):
            cc = pl.ds(al(c * q, q), q)
            got = nn(block, pc[r, cc])
            if first:
                acc[:, cc] = got
            else:
                acc[:, cc] += got
            return 0

        lax.fori_loop(0, hw // q, body, 0)
        got = nn(block, m[r, pl.ds(w + q, q)])
        if first:
            moved[...] = got
        else:
            moved[...] += got

    lax.fori_loop(0, hw // BLK, mask_rows, 0)
    build(z)
    pick(z, True, x_ref)
    build(zr(-1))
    build(zr(1))
    for s in range(4):
        came = ag_step(0, xbuf, x_ref, s)
        if s == 0:
            lax.fori_loop(0, 2 * hw // BLK, mask_rows_proj, 0)
        if s < 2:
            build(zr(-2 - s))
            build(zr(2 + s))
        elif s == 2:
            build(zr(4))
        for origin in came:
            pick(origin, False, xbuf.at[origin])
    cond[...] = acc[...].astype(BF16)

    pre[...] = nn(cond[...], lift[...])
    squash = jax.nn.sigmoid(pre[...])
    slope[...] = squash * (1.0 + pre[...] * (1.0 - squash))
    hid_ref[y, x] = (pre[...] * squash).astype(BF16)
    xy_tick(0, hid_ref, 0)

    def cond_copy(o):
        oy, ox = o // NR, o % NR
        ty, tx = lax.rem(y + oy, NR), lax.rem(x + ox, NR)
        return remote(
            cond.at[:, pl.ds(al((ty * NR + tx) * BLK, BLK), BLK)],
            condc_ref.at[me],
            a_s.at[o],
            a_r.at[o],
            dp_0=ty,
            dp_1=tx,
        )

    def cond_wait(o):
        oy, ox = o // NR, o % NR
        fy, fx = lax.rem(y + NR - oy, NR), lax.rem(x + NR - ox, NR)
        ref = condc_ref.at[fy * NR + fx]
        remote(ref, ref, a_s.at[o], a_r.at[o], dp_0=fy, dp_1=fx).wait_recv()

    for o in range(1, NR * NR):
        cond_copy(o).start()
    condc_ref[me] = cond[:, pl.ds(al(me * BLK, BLK), BLK)]

    hidden = hid_ref[y, x]

    def proj_rows(d, k):
        return pl.ds(al(k * hw + d * q, q), q)

    def shared_part(d):
        return jnp.concatenate(
            [nt(hidden, proj[proj_rows(d, 0), :]), nt(hidden, proj[proj_rows(d, 1), :])], axis=1
        )

    def spread(i):
        r = pl.ds(al(i * w, w), w)
        m[r, pl.ds(0, w)] = nn(pc[r, :], lift[...]).astype(BF16)

    def shared_tick(s):
        spread(s - 1)

    shared = rs(0, shared_part, shared_tick)
    xy_tick(0, hid_ref, 1)
    raw = shared[:, :q] + 2.0
    shift = shared[:, q:]
    scale = jax.nn.sigmoid(raw)
    keep_part = 1.0 - scale
    logs = jnp.minimum(raw, 0.0) - jnp.log1p(jnp.exp(-jnp.abs(raw)))
    logp_ref[...] = jnp.sum(logs.reshape(tok // 8, 8, q), axis=0)
    acc[:, pl.ds(0, q)] = scale
    acc[:, pl.ds(q, q)] = moved[...] + shift
    spread(3)
    xy_tick(0, hid_ref, 2)

    @pl.when(core == 1)
    def _():
        for k in (0, 1):

            @pl.when(4 * k + z // 2 != z)
            def _():
                ref = cbuf.at[:, pl.ds(k * q, q)]
                remote(ref, ref, cs.at[0], cr.at[k], tensor=z).wait_recv()

        cown[...] = cbuf[...]

    def hand():
        return remote(c0buf, c0buf, hs, hr, layers=1 - core)

    def gsend(k):
        dest = 4 * k + z // 2
        return remote(
            cown.at[:, pl.ds(k * q, q)],
            gbuf.at[:, pl.ds(al(lax.rem(z, 2) * q, q), q)],
            gs.at[k],
            gr.at[lax.rem(z, 2)],
            tensor=dest,
        )

    @pl.when(core == 0)
    def _():
        remote(gbuf, c0buf, hs, hr, layers=1 - core).wait_recv()
        cown[...] = c0buf[...]

    ca = cown[:, pl.ds(0, q)]
    cb = cown[:, pl.ds(q, q)].astype(F32)
    scale = acc[:, pl.ds(0, q)]
    keep_part = 1.0 - scale
    shift_grad = (cb * scale).astype(BF16)
    raw_grad = (cb * acc[:, pl.ds(q, q)] * scale * keep_part - keep_part).astype(BF16)
    stbuf[z, :, pl.ds(0, q)] = raw_grad
    stbuf[z, :, pl.ds(q, q)] = shift_grad
    own_st = stbuf.at[z]
    ag_start(1, stbuf, own_st)

    def st_piece(origin, k):
        return stbuf.at[origin, :, pl.ds(k * q, q)]

    def st_copy(origin, k):
        to = origin + NZ * k
        return remote(
            st_piece(origin, k), stc_ref.at[me], ts.at[to], tr.at[me], dp_0=to // NR, dp_1=lax.rem(to, NR)
        )

    def st_send(origin):
        for k in (0, 1):

            @pl.when(origin + NZ * k != me)
            def _():
                st_copy(origin, k).start()

            @pl.when(origin + NZ * k == me)
            def _():
                stc_ref[me] = stbuf[origin, :, pl.ds(k * q, q)]

    def act(origin):
        return nn(stbuf[origin, :, pl.ds(0, q)], proj[proj_rows(origin, 0), :]) + nn(
            stbuf[origin, :, pl.ds(q, q)], proj[proj_rows(origin, 1), :]
        )

    pre[...] = act(z)
    st_send(z)
    spread(4)
    for s in range(4):
        came = ag_step(1, stbuf, own_st, s)
        for origin in came:
            st_send(origin)
        if s < 3:
            spread(5 + s)
        for origin in came:
            pre[...] += act(origin)
        if s == 1:
            xy_tick(0, hid_ref, 3)
    grad_pre = (pre[...] * slope[...]).astype(BF16)
    gp_ref[y, x] = grad_pre
    xy_tick(0, hid_ref, 4)
    xy_tick(1, gp_ref, 0)

    lhs = jnp.concatenate([grad_pre, ca, shift_grad], axis=1)

    def in_rows(d, k):
        there = jnp.where(core == 1, k * hw + d * q, (2 * d + k) * q)
        return pl.ds(al(there, q), q)

    def in_part(d):
        return jnp.concatenate([nt(lhs, m[in_rows(d, 0), :]), nt(lhs, m[in_rows(d, 1), :])], axis=1)

    def in_tick(s):
        xy_tick(1, gp_ref, s)

    got = rs(1, in_part, in_tick)

    @pl.when(core == 1)
    def _():
        cown[...] = got.astype(BF16)
        remote(cown, c0buf, hs, hr, layers=1 - core).start()
        for k in (0, 1):

            @pl.when(4 * k + z // 2 != z)
            def _():
                gsend(k).start()

            @pl.when(4 * k + z // 2 == z)
            def _():
                gbuf[:, pl.ds(al(lax.rem(z, 2) * q, q), q)] = cown[:, pl.ds(k * q, q)]

    @pl.when(core == 0)
    def _():
        gin_ref[...] = got

    xy_tick(1, gp_ref, 4)

    @pl.when(core == 1)
    def _():
        for e in (0, 1):

            @pl.when(lax.rem(2 * z + e, NZ) != z)
            def _():
                ref = gbuf.at[:, pl.ds(e * q, q)]
                remote(ref, ref, gs.at[0], gr.at[e], tensor=z).wait_recv()

        gin_ref[...] = gbuf[...].astype(F32)
        remote(cown, c0buf, hs, hr, layers=1 - core).wait_send()
        for k in (0, 1):

            @pl.when(4 * k + z // 2 != z)
            def _():
                gsend(k).wait_send()

        for e in (0, 1):
            dest = lax.rem(2 * z + e, NZ)

            @pl.when(dest != z)
            def _():
                ref = cot_ref.at[:, pl.ds(e * q, q)]
                remote(ref, ref, cs.at[e], cr.at[0], tensor=dest).wait_send()

    for o in range(1, NR * NR):
        cond_wait(o)
        cond_copy(o).wait_send()

    def st_end(i, _):
        @pl.when(i != me)
        def _():
            ref = stc_ref.at[i]
            remote(ref, ref, ts.at[i], tr.at[i], dp_0=i // NR, dp_1=lax.rem(i, NR)).wait_recv()
            remote(ref, ref, ts.at[i], tr.at[i], dp_0=i // NR, dp_1=lax.rem(i, NR)).wait_send()

        return 0

    lax.fori_loop(0, NR * NR, st_end, 0)
    ag_finish(0, xbuf, x_ref)
    ag_finish(1, stbuf, own_st)
    rs_finish(0)
    rs_finish(1)
    xy_finish(0, hid_ref)
    xy_finish(1, gp_ref)


def token_side(x, cot, lift_w, proj_w, lmask, pmask, perm):
    tok, w = x.shape
    hw = lift_w.shape[0]
    feat = 2 * hw
    q = w // 2
    dma = pltpu.SemaphoreType.DMA
    vm = pl.BlockSpec(memory_space=pltpu.VMEM)
    sm = pl.BlockSpec(memory_space=pltpu.SMEM)
    n = NR * NR
    return pl.pallas_call(
        token_kernel,
        out_shape=(
            jax.ShapeDtypeStruct((tok, w), F32),
            jax.ShapeDtypeStruct((8, q), F32),
            jax.ShapeDtypeStruct((n, tok, BLK), BF16),
            jax.ShapeDtypeStruct((n, tok, q), BF16),
            jax.ShapeDtypeStruct((NR, NR, tok, w), BF16),
            jax.ShapeDtypeStruct((NR, NR, tok, w), BF16),
        ),
        in_specs=[vm, vm, vm, vm, sm, sm, vm],
        out_specs=(vm,) * 6,
        scratch_shapes=[
            pltpu.VMEM((NZ, tok, w), BF16),
            pltpu.VMEM((feat, hw), BF16),
            pltpu.VMEM((feat, 2 * w), BF16),
            pltpu.VMEM((hw, w), BF16),
            pltpu.VMEM((feat, w), BF16),
            pltpu.VMEM((tok, hw), F32),
            pltpu.VMEM((tok, hw), BF16),
            pltpu.VMEM((tok, q), F32),
            pltpu.VMEM((tok, w), F32),
            pltpu.VMEM((tok, w), F32),
            pltpu.VMEM((NZ, tok, w), BF16),
            pltpu.VMEM((2, 2, 4, tok, w), BF16),
            pltpu.VMEM((2, 2, 4, tok, w), BF16),
            pltpu.VMEM((tok, w), BF16),
            pltpu.VMEM((tok, w), BF16),
            pltpu.VMEM((tok, w), BF16),
            pltpu.VMEM((tok, w), BF16),
            dma((2, 2, 4, 2)),
            dma((2, 2, 4, 2)),
            dma((2, 2, 4, 2)),
            dma((2, 2, 4, 2)),
            dma((2,)),
            dma((2,)),
            dma((2,)),
            dma((2,)),
            dma,
            dma,
            dma((n,)),
            dma((n,)),
            dma((n,)),
            dma((n,)),
            dma((2, 2, 2, 2, 2)),
            dma((2, 2, 2, 2, 2)),
        ],
        compiler_params=pltpu.CompilerParams(
            collective_id=0, has_side_effects=True, vmem_limit_bytes=64 * 1024 * 1024 - 64 * 1024
        ),
        name="token_side",
    )(x, cot, lift_w, proj_w, lmask, pmask, perm)


def sum_kernel(v_ref, out_ref, zbuf, pbuf, mid, last, zs, zrv, ps, prv, ls, lr):
    z = lax.axis_index("tensor")
    y = lax.axis_index("dp_0")
    x = lax.axis_index("dp_1")
    core = lax.axis_index("layers")
    me = y * NR + x
    bar = pltpu.get_barrier_semaphore()
    for i in range(1, NZ):
        pl.semaphore_signal(bar, inc=1, device_id={"tensor": lax.rem(z + i, NZ)}, device_id_type=MESH)
    for o in range(1, NR * NR):
        ty, tx = lax.rem(y + o // NR, NR), lax.rem(x + o % NR, NR)
        pl.semaphore_signal(bar, inc=1, device_id={"dp_0": ty, "dp_1": tx}, device_id_type=MESH)
    pl.semaphore_signal(bar, inc=1, device_id={"layers": 1 - core}, device_id_type=MESH)
    pl.semaphore_wait(bar, NZ - 1 + NR * NR - 1 + 1)

    def zcopy(i):
        return remote(v_ref, zbuf.at[z], zs.at[i], zrv.at[i], tensor=lax.rem(z + i, NZ))

    for i in range(1, NZ):
        zcopy(i).start()
    zbuf[z] = v_ref[...]
    for i in range(1, NZ):
        ref = zbuf.at[lax.rem(z + NZ - i, NZ)]
        remote(ref, ref, zs.at[i], zrv.at[i], tensor=z).wait_recv()
    mid[...] = jnp.sum(zbuf[...], axis=0)

    def pcopy(o):
        ty, tx = lax.rem(y + o // NR, NR), lax.rem(x + o % NR, NR)
        return remote(mid, pbuf.at[me], ps.at[o], prv.at[o], dp_0=ty, dp_1=tx)

    for o in range(1, NR * NR):
        pcopy(o).start()
    pbuf[me] = mid[...]
    for o in range(1, NR * NR):
        fy, fx = lax.rem(y + NR - o // NR, NR), lax.rem(x + NR - o % NR, NR)
        ref = pbuf.at[fy * NR + fx]
        remote(ref, ref, ps.at[o], prv.at[o], dp_0=fy, dp_1=fx).wait_recv()
    last[0] = jnp.sum(pbuf[...], axis=0)
    swap = remote(last.at[0], last.at[1], ls, lr, layers=1 - core)
    swap.start()
    swap.wait_recv()
    out_ref[...] = last[0] + last[1]
    swap.wait_send()
    for i in range(1, NZ):
        zcopy(i).wait_send()
    for o in range(1, NR * NR):
        pcopy(o).wait_send()


def sum_all(v):
    dma = pltpu.SemaphoreType.DMA
    vm = pl.BlockSpec(memory_space=pltpu.VMEM)
    n = NR * NR
    return pl.pallas_call(
        sum_kernel,
        out_shape=jax.ShapeDtypeStruct(v.shape, F32),
        in_specs=[vm],
        out_specs=vm,
        scratch_shapes=[
            pltpu.VMEM((NZ,) + v.shape, F32),
            pltpu.VMEM((n,) + v.shape, F32),
            pltpu.VMEM(v.shape, F32),
            pltpu.VMEM((2,) + v.shape, F32),
            dma((NZ,)),
            dma((NZ,)),
            dma((n,)),
            dma((n,)),
            dma,
            dma,
        ],
        compiler_params=pltpu.CompilerParams(collective_id=1, has_side_effects=True),
        name="sum_all",
    )(v)


def expand_blocks(block_mask):
    blk_rows, blk_cols = block_mask.shape
    widened = jnp.broadcast_to((block_mask > 0)[:, None, :, None], (blk_rows, BLK, blk_cols, BLK))
    return widened.reshape(blk_rows * BLK, blk_cols * BLK)


def adam_step(gradient, kept, moment, square, factor):
    scaled = gradient * factor
    new_first = jnp.where(kept, beta_one * moment + (1.0 - beta_one) * scaled, moment)
    new_second = jnp.where(kept, beta_two * square + (1.0 - beta_two) * scaled * scaled, square)
    bias_one = 1.0 - beta_one**ADAM_STEP
    bias_two = 1.0 - beta_two**ADAM_STEP
    update = jnp.where(
        kept, new_first / bias_one / (jnp.sqrt(new_second / bias_two) + adam_eps), 0.0
    )
    return (new_first[None], new_second[None], update[None])


def per_device(
    section_input,
    out_cotangent,
    lift_weight,
    proj_weight,
    lift_mask,
    proj_mask,
    channel_perm,
    lift_moment,
    lift_square,
    proj_moment,
    proj_square,
):
    core = lax.axis_index("layers")
    dp_index = lax.axis_index(DP)
    gin, logp, condc, stc, hid, gp = token_side(
        section_input[0],
        out_cotangent,
        lift_weight[0],
        proj_weight[0],
        lift_mask[0],
        proj_mask[0],
        channel_perm,
    )
    n, tok, _ = condc.shape
    tokens = n * tok
    w = gin.shape[1]
    lift_grad = tn(condc.reshape(tokens, -1), gp.reshape(tokens, w))
    proj_grad = tn(stc.reshape(tokens, -1), hid.reshape(tokens, w))
    lift_rows = lift_moment.shape[1] // BLK
    proj_rows = proj_moment.shape[1] // BLK
    lift_own = expand_blocks(lax.dynamic_slice_in_dim(lift_mask[0], dp_index * lift_rows, lift_rows, 0))
    proj_own = expand_blocks(lax.dynamic_slice_in_dim(proj_mask[0], dp_index * proj_rows, proj_rows, 0))
    lift_grad = jnp.where(lift_own, lift_grad, 0.0)
    proj_grad = jnp.where(proj_own, proj_grad, 0.0)
    local_sq = jnp.sum(lift_grad * lift_grad) + jnp.sum(proj_grad * proj_grad)
    lane = lax.broadcasted_iota(jnp.int32, (8, BLK), 1)
    row = lax.broadcasted_iota(jnp.int32, (8, BLK), 0)
    first = row == 0
    packed = jnp.where(first & (lane == 0), local_sq, 0.0) + jnp.where(
        first & (lane == 1 + core), jnp.sum(logp), 0.0
    )
    sums = sum_all(packed)
    factor = jnp.minimum(1.0, CLIP / (jnp.sqrt(sums[0, 0]) + 1e-06))
    log_total = jnp.where(core == 0, sums[0, 1], sums[0, 2])
    lift_out = adam_step(lift_grad, lift_own, lift_moment[0], lift_square[0], factor)
    proj_out = adam_step(proj_grad, proj_own, proj_moment[0], proj_square[0], factor)
    log_det = (log_total / (tokens * lift_weight.shape[1])).reshape(1)
    return (gin[None], log_det) + lift_out + proj_out


def solution(mesh):
    finer = Mesh(
        mesh.devices.reshape(NR, NR, mesh.shape["tensor"], mesh.shape["layers"]),
        ("dp_0", "dp_1", "tensor", "layers"),
    )
    tiled = P("layers", DP, "tensor")
    weight = P("layers", None, "tensor")
    return jax.shard_map(
        per_device,
        mesh=finer,
        in_specs=(tiled, P(DP, "tensor")) + (weight,) * 4 + (P("layers", None),) + (tiled,) * 4,
        out_specs=(tiled, P("layers")) + (tiled,) * 6,
        check_vma=False,
    )
```

time: 440 us -> 166 us (0.38)
  waiting for transfers between devices: 241 us -> 0 us
  Pallas kernels: 0 us -> 143 us
  local copies, waits for them, and re-layouts: 66.6 us -> 5.17 us
  blocking collectives: 41.7 us -> 0 us
  other arithmetic: 32.9 us -> 6.12 us
  starting transfers between devices: 17 us -> 0 us
  matrix products: 20.9 us -> 6 us
  between operations: 18.8 us -> 5.22 us
    all_gather x4 -> x0, waiting for transfers between devices: 165 us -> none  [the longest x2 84.9 us: side_by_side(): lax.all_gather(both, axis, axis=dim, tiled=True)]
    pallas_call x0 -> x2, Pallas kernels: none -> 143 us  [the longest x1 97.8 us: token_side(): pl.pallas_call(token_kernel, out_shape=(jax.ShapeDtypeStruct((tok, w), F3...]
    psum x1 -> x0, waiting for transfers between devices: 74.5 us -> none  [per_device(): lax.psum(contract_cols(hidden, proj_eff).astype(jnp.bfloat16), 'tensor')]
    psum x4 -> x0, blocking collectives: 41.7 us -> none  [over_axes(): return functools.reduce(lax.psum, axes, array)]
    gather x5 -> x0, local copies, waits for them, and re-layouts: 31.8 us -> none  [the longest x2 16.5 us: per_device(): early_grad = jnp.take(early_mixed, inverse, axis=1)]
    scatter x1 -> x0, local copies, waits for them, and re-layouts: 15.5 us -> none  [per_device(): inverse = jnp.zeros((feat_width,), jnp.int32).at[channel_order].set(jnp.a...]
    dot_general x7 -> x2, matrix products: 20.9 us -> 6 us  [tn(): lax.dot_general(a, b, (((0,), (0,)), ((), ())), preferred_element_type=F32)]
    all_to_all x2 -> x0, starting transfers between devices: 13.1 us -> none  [the longest x1 6.54 us: per_device(): lax.all_to_all(cond_side, DP, split_axis=1, concat_axis=0, tiled=True)]
  transfers between devices with their start and end apart: 8 -> 0, of which waited for: 6 -> 0; matrix products, arithmetic and copies ran while one was open for 9% -> 0% of each run, Pallas kernels for 0% -> 0%
where the time goes in v1:
time: 166 us
  Pallas kernels  143 us (86%)
  other arithmetic  6.12 us (4%)
  matrix products  6 us (4%)
  between operations  5.22 us (3%)
  local copies, waits for them, and re-layouts  5.17 us (3%)
    pallas_call x1, Pallas kernels, token_side(): pl.pallas_call(token_kernel, out_shape=(jax.ShapeDtypeStruct((tok, w), F3...  97.8 us
    pallas_call x1, Pallas kernels, sum_all(): pl.pallas_call(sum_kernel, out_shape=jax.ShapeDtypeStruct(v.shape, F32),...  45.6 us
    dot_general x2, matrix products, tn(): lax.dot_general(a, b, (((0,), (0,)), ((), ())), preferred_element_type=F32)  6 us

profile of v1, /device:TPU:1, one launch (start us, length us, event | category | flops | bytes accessed | tf_op | source)
XLA Modules:
  0.0 165.9 jit_solution(5252505368135390302)
XLA Ops:
  0.6 1.4 copy.19.lmask_ref
  2.0 1.4 copy.20.pmask_ref
  3.4 97.8 %token_side.1 = (f32[128,512]{1,0:T(8,128)}, f32[8,256]{1,0:T(8,128)}, bf16[16,128,128]{2,1,0:T(8,128)(2,1)}, bf16[16,128,256]{2,1,0:T(8,128)(2,1)}, bf16[4,4,12...) custom-call(bf16[128,512]{1,0:T(8,128)(2,1)} %bitcast.95, bf16[128,512]{1,0:T(8,128)(2,1)} %cot_ref.1, ...), custom_call_target="tpu_custom_call" | custom-call | tf_op jit(solution)/shard_map/token_side/pallas_call | solution.py:579
  101.2 0.0 copy-start.5
  101.2 0.0 copy-start.6
  101.2 1.4 reduce_sum.29
  102.6 0.9 fusion.10
  103.5 0.1 broadcast_bitcast_fusion
  103.5 2.9 %multiply_reduce_fusion.1 = (f32[]{:T(128)}, f32[128,512]{1,0:T(8,128)S(1)}) fusion(bf16[2048,128]{1,0:T(8,128)(2,1)} %bitcast.93, bf16[2048,512]{1,0:T(8,128)(2,1)} %bitcast.90, pred[512]{0:T(512)(128)(4,1)S(1)} %broadcast_bitcast_fusion), kind=kOutput, calls=%fused_computation.19 | convolution fusion | flops 268632064 | bytes 2884100 | tf_op jit(solution)/shard_map/dot_general | solution.py:34
  106.4 0.0 copy-done.5
  106.4 0.1 dynamic-slice_compare_fusion
  106.5 0.1 copy.21
  106.6 0.1 broadcast_in_dim.64
  106.7 0.0 copy-done.6
  106.8 0.0 copy-start.3
  106.8 0.0 copy-start.4
  106.8 0.0 copy-start
  106.8 0.0 copy-start.1
  106.8 3.1 %multiply_reduce_fusion = (f32[]{:T(128)}, f32[256,512]{1,0:T(8,128)S(1)}) fusion(bf16[2048,256]{1,0:T(8,128)(2,1)S(1)} %bitcast.100, bf16[2048,512]{1,0:T(8,128)(2,1)} %bitcast.99, pred[32,8,4,128]{3,2,1,0:T(4,128)(4,1)S(1)} %bitcast.91), kind=kOutput, calls=%fused_computation.10 | convolution fusion | flops 537264128 | bytes 3801092 | tf_op jit(solution)/shard_map/dot_general | solution.py:34
  111.3 1.3 select_add_fusion.v_ref
  112.6 45.6 %sum_all.1 = f32[8,128]{1,0:T(8,128)} custom-call(f32[8,128]{1,0:T(8,128)} %select_add_fusion.v_ref), custom_call_target="tpu_custom_call" | custom-call | tf_op jit(solution)/shard_map/sum_all/pallas_call | solution.py:686
  158.2 1.4 fusion.11
  161.6 0.0 copy-done.3
  161.6 0.0 copy-done.4
  161.6 0.0 copy-start.2
  161.6 1.0 select_bitcast_fusion.1
  162.6 0.0 copy-done
  162.6 0.0 copy-done.1
  162.6 1.5 select_bitcast_fusion
  164.1 0.0 copy-done.2
  164.1 0.7 copy.36
  (2 shorter events, 0.0 us)
Async XLA Ops:
  101.2 5.2 %copy-start.5 = (s32[1,32,4]{1,2,0:T(4,128)S(1)}, s32[1,32,4]{1,2,0:T(4,128)}, u32[]{:S(2)}) copy-start(s32[1,32,4]{1,2,0:T(4,128)} %param.16) | copy-start | bytes 1540
  101.2 5.6 %copy-start.6 = (bf16[16,128,256]{2,1,0:T(8,128)(2,1)S(1)}, bf16[16,128,256]{2,1,0:T(8,128)(2,1)}, u32[]{:S(2)}) copy-start(bf16[16,128,256]{2,1,0:T(8,128)(2,1)} %get-tuple-element.17) | copy-start | bytes 3145732
  106.8 54.9 %copy-start.3 = (f32[1,128,512]{2,1,0:T(8,128)S(1)}, f32[1,128,512]{2,1,0:T(8,128)}, u32[]{:S(2)}) copy-start(f32[1,128,512]{2,1,0:T(8,128)} %param.18) | copy-start | bytes 786436
  106.8 54.8 %copy-start.4 = (f32[1,128,512]{2,1,0:T(8,128)S(1)}, f32[1,128,512]{2,1,0:T(8,128)}, u32[]{:S(2)}) copy-start(f32[1,128,512]{2,1,0:T(8,128)} %param.19) | copy-start | bytes 786436
  106.8 55.9 %copy-start = (f32[1,256,512]{2,1,0:T(8,128)S(1)}, f32[1,256,512]{2,1,0:T(8,128)}, u32[]{:S(2)}) copy-start(f32[1,256,512]{2,1,0:T(8,128)} %param.20) | copy-start | bytes 1572868
  106.8 55.9 %copy-start.1 = (f32[1,256,512]{2,1,0:T(8,128)S(1)}, f32[1,256,512]{2,1,0:T(8,128)}, u32[]{:S(2)}) copy-start(f32[1,256,512]{2,1,0:T(8,128)} %param.21) | copy-start | bytes 1572868
  161.6 2.5 %copy-start.2 = (f32[128,512]{1,0:T(8,128)S(1)}, f32[128,512]{1,0:T(8,128)}, u32[]{:S(2)}) copy-start(f32[128,512]{1,0:T(8,128)} %get-tuple-element.14) | copy-start | bytes 786436

commit v2 on v1

v2 whole, which is shorter than its diff:
```python
import functools

import jax
import jax.numpy as jnp
from jax import lax
from jax.experimental import pallas as pl
from jax.experimental.pallas import tpu as pltpu
from jax.sharding import Mesh
from jax.sharding import PartitionSpec as P

BLK = 128
ADAM_STEP = 10
CLIP = 4096
DP = ("dp_0", "dp_1")
MESH = pl.DeviceIdType.MESH
F32 = jnp.float32
BF16 = jnp.bfloat16

NZ = 8
NR = 4
NQ = 4

beta_one = 0.9
beta_two = 0.99
adam_eps = 1e-08


def nn(a, b):
    return jnp.dot(a, b, preferred_element_type=F32)


def nt(a, b):
    return lax.dot_general(a, b, (((1,), (1,)), ((), ())), preferred_element_type=F32)


def tn(a, b):
    return lax.dot_general(a, b, (((0,), (0,)), ((), ())), preferred_element_type=F32)


def al(i, m):
    return pl.multiple_of(i, m)


def remote(src, dst, ssem, rsem, **where):
    return pltpu.make_async_remote_copy(
        src_ref=src, dst_ref=dst, send_sem=ssem, recv_sem=rsem, device_id=where, device_id_type=MESH
    )


def far(d, h):
    return (h < NQ // 2) == (d == 0)


def both_ways(d, s, h):
    return s < 3 or far(d, h)


FIRST = [sorted(range(NQ), key=lambda h: not far(d, h)) for d in (0, 1)]
LAST = [sorted(range(NQ), key=lambda h: far(d, h)) for d in (0, 1)]


def token_kernel(
    x_ref,
    cot_ref,
    lift_hbm,
    proj_hbm,
    lmask_ref,
    pmask_ref,
    perm_ref,
    gin_out,
    stat_ref,
    lgrad_out,
    pgrad_out,
    xbuf,
    pc,
    m,
    lift,
    proj,
    cond,
    sm,
    slope,
    pre,
    stbuf,
    sbuf,
    rbuf,
    cbuf,
    c0buf,
    gbuf,
    cown,
    condc_ref,
    stc_ref,
    hid_ref,
    gp_ref,
    vec,
    zbuf,
    mid,
    pbuf,
    other,
    gin_ref,
    lgrad_ref,
    pgrad_ref,
    w_s,
    o_s,
    ag_s,
    ag_r,
    rs_s,
    rs_r,
    cs,
    cr,
    gs,
    gr,
    hs,
    hr,
    a_s,
    a_r,
    ts,
    tr,
    xs,
    xr,
    zs,
    zrv,
    ps,
    prv,
    ls,
    lr,
):
    z = lax.axis_index("tensor")
    y = lax.axis_index("dp_0")
    x = lax.axis_index("dp_1")
    core = lax.axis_index("layers")
    me = y * NR + x
    tok = x_ref.shape[0]
    half = tok // 2
    quart = tok // 4
    w = x_ref.shape[1]
    q = w // 2
    hw = NZ * q

    nq = tok // NQ

    def rows(h):
        return pl.ds(h * nq, nq)

    def zr(i):
        return lax.rem(z + NZ + i, NZ)

    zside = (zr(1), zr(-1))
    load_lift = pltpu.make_async_copy(lift_hbm, lift, w_s.at[0])
    load_proj = pltpu.make_async_copy(proj_hbm, proj, w_s.at[1])
    load_lift.start()
    load_proj.start()

    bar = pltpu.get_barrier_semaphore()
    for i in range(1, NZ):
        pl.semaphore_signal(bar, inc=1, device_id={"tensor": zr(i)}, device_id_type=MESH)
    for oy in range(NR):
        for ox in range(NR):
            if oy or ox:
                pl.semaphore_signal(
                    bar,
                    inc=1,
                    device_id={"dp_0": lax.rem(y + oy, NR), "dp_1": lax.rem(x + ox, NR)},
                    device_id_type=MESH,
                )
    pl.semaphore_signal(bar, inc=1, device_id={"layers": 1 - core}, device_id_type=MESH)

    def ag_copy(p, buf, own, s, d, h):
        origin = zr(-s) if d == 0 else zr(s)
        src = own.at[rows(h)] if s == 0 else buf.at[origin, rows(h)]
        return remote(src, buf.at[origin, rows(h)], ag_s.at[d, s, h], ag_r.at[d, s, h], tensor=zside[d])

    def ag_wait(p, buf, s, d, h):
        origin = zr(-1 - s) if d == 0 else zr(1 + s)
        ref = buf.at[origin, rows(h)]
        remote(ref, ref, ag_s.at[d, s, h], ag_r.at[d, s, h], tensor=zside[d]).wait_recv()

    def ag_start(p, buf, own):
        for k in range(NQ):
            for d in (0, 1):
                ag_copy(p, buf, own, 0, d, FIRST[d][k]).start()

    def ag_step(p, buf, own, s):
        for k in range(NQ):
            for d in (0, 1):
                h = FIRST[d][k]
                if both_ways(d, s, h):
                    ag_wait(p, buf, s, d, h)
                    if s < 3 and both_ways(d, s + 1, h):
                        ag_copy(p, buf, own, s + 1, d, h).start()
        return [zr(-1 - s), zr(1 + s)] if s < 3 else [zr(4)]

    def ag_finish(p, buf, own):
        for d in (0, 1):
            for s in range(4):
                for h in range(NQ):
                    if both_ways(d, s, h):
                        ag_copy(p, buf, own, s, d, h).wait_send()

    def rs_copy(p, s, d, h):
        return remote(
            sbuf.at[p, d, s, rows(h)],
            rbuf.at[p, d, s, rows(h)],
            rs_s.at[d, s, h],
            rs_r.at[d, s, h],
            tensor=zside[d],
        )

    def rs(p, part, tick):
        most = part(zr(4))
        for k in range(NQ // 2):
            for d in (0, 1):
                h = FIRST[d][k]
                sbuf[p, d, 0, rows(h)] = most[h * nq : (h + 1) * nq].astype(BF16)
                rs_copy(p, 0, d, h).start()
        for s in (1, 2, 3):
            mine = [part(zr(4 - s)), part(zr(s - 4))]

            def send(d, h, own):
                sbuf[p, d, s, rows(h)] = own.astype(BF16)
                rs_copy(p, s, d, h).start()

            if s == 1:
                for k in range(NQ // 2):
                    for d in (0, 1):
                        h = LAST[d][k]
                        send(d, h, mine[d][h * nq : (h + 1) * nq])
            with jax.named_scope(f"tick{s}"):
                tick(s)
            with jax.named_scope(f"w{s}"):
                for k in range(NQ // 2 if s == 1 else 0, NQ):
                    for d in (0, 1):
                        h = LAST[d][k]
                        rs_copy(p, s - 1, d, h).wait_recv()
                        own = mine[d][h * nq : (h + 1) * nq]
                        send(d, h, own + rbuf[p, d, s - 1, rows(h)].astype(F32))

        def end():
            own = part(z)
            with jax.named_scope("w4"):
                for d in (0, 1):
                    for h in range(NQ):
                        rs_copy(p, 3, d, h).wait_recv()
            return own + rbuf[p, 0, 3].astype(F32) + rbuf[p, 1, 3].astype(F32)

        return end

    def rs_finish(p):
        for d in (0, 1):
            for s in range(4):
                for h in range(NQ):
                    if s > 0 or far(d, h):
                        rs_copy(p, s, d, h).wait_send()

    def along(axis, i):
        if axis == "dp_1":
            return {"dp_1": lax.rem(x + NR + i, NR)}
        return {"dp_0": lax.rem(y + NR + i, NR)}

    def slot(buf, stage, h, off, r):
        axis = ("dp_1", "dp_0")[(h + stage) % 2]
        yy, xx = (y, lax.rem(x + NR + off, NR)) if axis == "dp_1" else (lax.rem(y + NR + off, NR), x)
        if stage == 0:
            return buf.at[yy, xx, r]
        return buf.at[yy, :, r] if axis == "dp_0" else buf.at[:, xx, r]

    def xy_rows(h, t, d):
        if t == 0:
            return pl.ds(h * half, half)
        return pl.ds(h * half + d * quart, quart)

    def xy_copy(p, buf, stage, h, t, d):
        axis = ("dp_1", "dp_0")[(h + stage) % 2]
        step = 1 if d == 0 else -1
        src = slot(buf, stage, h, 0 if t == 0 else -step, xy_rows(h, t, d))
        return remote(
            src, src, xs.at[p, stage, h, t, d], xr.at[p, stage, h, t, d], **along(axis, step)
        )

    def xy_wait(p, buf, stage, h, t, d):
        axis = ("dp_1", "dp_0")[(h + stage) % 2]
        step = 1 if d == 0 else -1
        ref = slot(buf, stage, h, -step if t == 0 else -2 * step, xy_rows(h, t, d))
        remote(
            ref, ref, xs.at[p, stage, h, t, d], xr.at[p, stage, h, t, d], **along(axis, step)
        ).wait_recv()

    def xy_tick(p, buf, k):
        stage, t = k // 2, k % 2
        with jax.named_scope(f"xy{p}{k}"):
            if k:
                ps_, pt = (k - 1) // 2, (k - 1) % 2
                for h in (0, 1):
                    for d in (0, 1):
                        xy_wait(p, buf, ps_, h, pt, d)
            if k < 4:
                for h in (0, 1):
                    for d in (0, 1):
                        xy_copy(p, buf, stage, h, t, d).start()

    def xy_finish(p, buf):
        for stage in (0, 1):
            for h in (0, 1):
                for t in (0, 1):
                    for d in (0, 1):
                        xy_copy(p, buf, stage, h, t, d).wait_send()

    def mask_lift(i, _):
        r = pl.ds(al(i * BLK, BLK), BLK)
        for c in range(w // BLK):
            cc = pl.ds(c * BLK, BLK)
            keep = lmask_ref[c, i].astype(F32)
            lift[r, cc] = (lift[r, cc].astype(F32) * keep).astype(BF16)
        return 0

    def mask_proj(i, _):
        r = pl.ds(al(i * BLK, BLK), BLK)
        for c in range(w // BLK):
            cc = pl.ds(c * BLK, BLK)
            keep = pmask_ref[c, i].astype(F32)
            proj[r, cc] = (proj[r, cc].astype(F32) * keep).astype(BF16)
        return 0

    ca_perm = pl.ds(al(z * q, q), q)
    mv_perm = pl.ds(al(hw + z * q, q), q)

    def hot(base, order):
        at = lax.broadcasted_iota(jnp.int32, (BLK, q), 0) + base
        return jnp.where(at == order, 1.0, 0.0).astype(BF16)

    def build(i, _):
        base = i * BLK
        r = pl.ds(al(base, BLK), BLK)
        for c in range(hw // q):
            cc = pl.ds(c * q, q)
            pc[r, cc] = hot(base, perm_ref[:, cc])
        m[r, pl.ds(w, q)] = hot(base, perm_ref[:, ca_perm])
        m[r, pl.ds(w + q, q)] = hot(base, perm_ref[:, mv_perm])
        return 0

    def of(origin):
        return pl.ds(al(origin * w, w), w)

    def spread(origin):
        with jax.named_scope("spread"):
            m[of(origin), pl.ds(0, w)] = nn(pc[of(origin), :], lift[...]).astype(BF16)

    def times(origin):
        return nn(xbuf[origin], m[of(origin), pl.ds(0, w)])

    def pick(c, _):
        cc = pl.ds(al(c * q, q), q)
        got = nn(xbuf[0], pc[pl.ds(0, w), cc])
        for o in range(1, NZ):
            got = got + nn(xbuf[o], pc[pl.ds(o * w, w), cc])
        cond[:, cc] = got.astype(BF16)
        return 0

    with jax.named_scope("build"):
        lax.fori_loop(0, 2 * hw // BLK, build, 0)
    xbuf[z] = x_ref[...]
    load_lift.wait()
    lax.fori_loop(0, hw // BLK, mask_lift, 0)
    spread(z)
    spread(zr(-1))
    with jax.named_scope("barrier"):
        pl.semaphore_wait(bar, NZ - 1 + NR * NR - 1 + 1)
    ag_start(0, xbuf, x_ref)

    @pl.when(core == 1)
    def _():
        for e in (0, 1):
            dest = lax.rem(2 * z + e, NZ)
            piece = cot_ref.at[:, pl.ds(e * q, q)]
            land = cbuf.at[:, pl.ds(al((z // 4) * q, q), q)]

            @pl.when(dest != z)
            def _():
                remote(piece, land, cs.at[e], cr.at[z // 4], tensor=dest).start()

            @pl.when(dest == z)
            def _():
                cbuf[:, pl.ds(al((z // 4) * q, q), q)] = cot_ref[:, pl.ds(e * q, q)]

    spread(zr(1))
    pre[...] = times(z)
    spread(zr(-2))
    spread(zr(2))
    load_proj.wait()
    with jax.named_scope("mask_proj"):
        lax.fori_loop(0, 2 * hw // BLK, mask_proj, 0)
    for s in range(4):
        with jax.named_scope(f"agx{s}"):
            came = ag_step(0, xbuf, x_ref, s)
        if s < 3:
            spread((zr(-3), zr(3), zr(4))[s])
        for origin in came:
            pre[...] += times(origin)

    ag_finish(0, xbuf, x_ref)

    squash = jax.nn.sigmoid(pre[...])
    slope[...] = squash * (1.0 + pre[...] * (1.0 - squash))
    hid_ref[y, x] = (pre[...] * squash).astype(BF16)
    xy_tick(0, hid_ref, 0)

    hidden = hid_ref[y, x]

    def proj_rows(d, k):
        return pl.ds(al(k * hw + d * q, q), q)

    def shared_part(d):
        return jnp.concatenate(
            [nt(hidden, proj[proj_rows(d, 0), :]), nt(hidden, proj[proj_rows(d, 1), :])], axis=1
        )

    def shared_tick(s):
        if s == 1:
            got = nn(xbuf[0], m[pl.ds(0, w), pl.ds(w + q, q)])
            for o in range(1, NZ):
                got = got + nn(xbuf[o], m[pl.ds(o * w, w), pl.ds(w + q, q)])
            sm[:, pl.ds(q, q)] = got

    with jax.named_scope("rs_shared"):
        shared = rs(0, shared_part, shared_tick)()
    rs_finish(0)
    raw = shared[:, :q] + 2.0
    scale = jax.nn.sigmoid(raw)
    sm[:, pl.ds(0, q)] = scale
    sm[:, pl.ds(q, q)] += shared[:, q:]
    logs = jnp.minimum(raw, 0.0) - jnp.log1p(jnp.exp(-jnp.abs(raw)))
    logs = jnp.sum(logs.reshape(tok // 8, 8, q), axis=0)
    vec[1] = logs[:, :BLK] + logs[:, BLK:]
    xy_tick(0, hid_ref, 1)

    def cond_copy(o):
        oy, ox = o // NR, o % NR
        ty, tx = lax.rem(y + oy, NR), lax.rem(x + ox, NR)
        return remote(
            cond.at[:, pl.ds(al((ty * NR + tx) * BLK, BLK), BLK)],
            condc_ref.at[me],
            a_s,
            a_r,
            dp_0=ty,
            dp_1=tx,
        )

    def all_of(buf, ssem, rsem):
        ref = buf.at[pl.ds(0, buf.shape[0] - 1)]
        return remote(ref, ref, ssem, rsem, dp_0=lax.rem(y + 1, NR))

    def permute_tokens(lo, hi):
        with jax.named_scope("permute"):
            lax.fori_loop(lo, hi, pick, 0)
        if hi == hw // q:
            for o in range(1, NR * NR):
                cond_copy(o).start()
            condc_ref[me] = cond[:, pl.ds(al(me * BLK, BLK), BLK)]

    @pl.when(core == 1)
    def _():
        for k in (0, 1):

            @pl.when(4 * k + z // 2 != z)
            def _():
                ref = cbuf.at[:, pl.ds(k * q, q)]
                remote(ref, ref, cs.at[0], cr.at[k], tensor=z).wait_recv()

        cown[...] = cbuf[...]

    @pl.when(core == 0)
    def _():
        permute_tokens(0, hw // q)
        xy_tick(0, hid_ref, 2)
        with jax.named_scope("handwait"):
            remote(gbuf, c0buf, hs, hr, layers=1 - core).wait_recv()
        cown[...] = c0buf[...]

    ca = cown[:, pl.ds(0, q)]
    cb = cown[:, pl.ds(q, q)].astype(F32)
    scale = sm[:, pl.ds(0, q)]
    keep_part = 1.0 - scale
    shift_grad = (cb * scale).astype(BF16)
    raw_grad = (cb * sm[:, pl.ds(q, q)] * scale * keep_part - keep_part).astype(BF16)
    stbuf[z, :, pl.ds(0, q)] = raw_grad
    stbuf[z, :, pl.ds(q, q)] = shift_grad
    own_st = stbuf.at[z]
    ag_start(1, stbuf, own_st)

    def st_copy(origin, k):
        to = origin + NZ * k
        return remote(
            stbuf.at[origin, :, pl.ds(k * q, q)],
            stc_ref.at[me],
            ts,
            tr,
            dp_0=to // NR,
            dp_1=lax.rem(to, NR),
        )

    def st_send(origin):
        for k in (0, 1):

            @pl.when(origin + NZ * k != me)
            def _():
                st_copy(origin, k).start()

            @pl.when(origin + NZ * k == me)
            def _():
                stc_ref[me] = stbuf[origin, :, pl.ds(k * q, q)]

    def act(origin):
        return nn(stbuf[origin, :, pl.ds(0, q)], proj[proj_rows(origin, 0), :]) + nn(
            stbuf[origin, :, pl.ds(q, q)], proj[proj_rows(origin, 1), :]
        )

    pre[...] = act(z)
    st_send(z)

    @pl.when(core == 1)
    def _():
        permute_tokens(0, 5)

    for s in range(4):
        with jax.named_scope(f"agst{s}"):
            came = ag_step(1, stbuf, own_st, s)
        if s < 2:
            for origin in came:
                st_send(origin)
        for origin in came:
            pre[...] += act(origin)
        if s == 0:

            @pl.when(core == 1)
            def _():
                permute_tokens(5, hw // q)

        if s == 1:

            @pl.when(core == 0)
            def _():
                xy_tick(0, hid_ref, 3)

        if s == 2:

            @pl.when(core == 1)
            def _():
                xy_tick(0, hid_ref, 2)

    grad_pre = (pre[...] * slope[...]).astype(BF16)
    gp_ref[y, x] = grad_pre
    xy_tick(1, gp_ref, 0)

    lhs = jnp.concatenate([grad_pre, ca, shift_grad], axis=1)

    def in_rows(d, k):
        there = jnp.where(core == 1, k * hw + d * q, (2 * d + k) * q)
        return pl.ds(al(there, q), q)

    def in_part(d):
        return jnp.concatenate([nt(lhs, m[in_rows(d, 0), :]), nt(lhs, m[in_rows(d, 1), :])], axis=1)

    def in_tick(s):
        @pl.when(core == 0)
        def _():
            xy_tick(1, gp_ref, s)

        if s == 1:
            for i in (-3, 3, 4):
                st_send(zr(i))

    with jax.named_scope("rs_in"):
        end = rs(1, in_part, in_tick)

    def gsend(k):
        return remote(
            cown.at[:, pl.ds(k * q, q)],
            gbuf.at[:, pl.ds(al(lax.rem(z, 2) * q, q), q)],
            gs.at[k],
            gr.at[lax.rem(z, 2)],
            tensor=4 * k + z // 2,
        )

    @pl.when(core == 1)
    def _():
        cown[...] = end().astype(BF16)
        remote(cown, c0buf, hs, hr, layers=1 - core).start()
        for k in (0, 1):

            @pl.when(4 * k + z // 2 != z)
            def _():
                gsend(k).start()

            @pl.when(4 * k + z // 2 == z)
            def _():
                gbuf[:, pl.ds(al(lax.rem(z, 2) * q, q), q)] = cown[:, pl.ds(k * q, q)]

        xy_tick(1, gp_ref, 1)
        xy_tick(0, hid_ref, 3)
        xy_tick(1, gp_ref, 2)
        xy_tick(0, hid_ref, 4)
        xy_tick(1, gp_ref, 3)

    tokens = NR * NR * tok

    def squares(g):
        g = jnp.sum((g * g).reshape(g.shape[0] // 8, 8, w), axis=0)
        out = g[:, :BLK]
        for c in range(1, w // BLK):
            out = out + g[:, c * BLK : (c + 1) * BLK]
        return out

    @pl.when(core == 0)
    def _():
        xy_tick(0, hid_ref, 4)

    with jax.named_scope("stcome"):
        all_of(stc_ref, ts, tr).wait_recv()
    with jax.named_scope("pgrad"):
        pgrad_ref[...] = tn(stc_ref[...].reshape(tokens, q), hid_ref[...].reshape(tokens, w))
    for b in range(q // BLK):
        for c in range(w // BLK):
            keep = pmask_ref[c, me * (q // BLK) + b].astype(F32)
            pgrad_ref[pl.ds(b * BLK, BLK), pl.ds(c * BLK, BLK)] *= keep
    vec[0] = squares(pgrad_ref[...])
    with jax.named_scope("condwait"):
        all_of(condc_ref, a_s, a_r).wait_recv()
    xy_tick(1, gp_ref, 4)
    with jax.named_scope("lgrad"):
        lgrad_ref[...] = tn(condc_ref[...].reshape(tokens, BLK), gp_ref[...].reshape(tokens, w))
    for c in range(w // BLK):
        keep = lmask_ref[c, me].astype(F32)
        lgrad_ref[:, pl.ds(c * BLK, BLK)] *= keep
    vec[0] += squares(lgrad_ref[...])

    save_pgrad = pltpu.make_async_copy(pgrad_ref, pgrad_out, o_s.at[0])
    save_lgrad = pltpu.make_async_copy(lgrad_ref, lgrad_out, o_s.at[1])
    save_gin = pltpu.make_async_copy(gin_ref, gin_out, o_s.at[2])
    def zcopy(i):
        return remote(vec, zbuf.at[z], zs, zrv, tensor=zr(i))

    for i in range(1, NZ):
        zcopy(i).start()
    zbuf[z] = vec[...]
    save_pgrad.start()
    save_lgrad.start()

    @pl.when(core == 1)
    def _():
        for e in (0, 1):

            @pl.when(lax.rem(2 * z + e, NZ) != z)
            def _():
                ref = gbuf.at[:, pl.ds(e * q, q)]
                remote(ref, ref, gs.at[0], gr.at[e], tensor=z).wait_recv()

        gin_ref[...] = gbuf[...].astype(F32)

    @pl.when(core == 0)
    def _():
        gin_ref[...] = end()

    save_gin.start()
    with jax.named_scope("zsum"):
        all_of(zbuf, zs, zrv).wait_recv()
    mid[...] = jnp.sum(zbuf[...], axis=0)

    def pcopy(o):
        ty, tx = lax.rem(y + o // NR, NR), lax.rem(x + o % NR, NR)
        return remote(mid, pbuf.at[me], ps, prv, dp_0=ty, dp_1=tx)

    for o in range(1, NR * NR):
        pcopy(o).start()
    pbuf[me] = mid[...]
    with jax.named_scope("psum"):
        all_of(pbuf, ps, prv).wait_recv()
    other[0] = jnp.sum(pbuf[...], axis=0)
    swap = remote(other.at[0], other.at[1], ls, lr, layers=1 - core)
    swap.start()

    @pl.when(core == 1)
    def _():
        remote(cown, c0buf, hs, hr, layers=1 - core).wait_send()
        for k in (0, 1):

            @pl.when(4 * k + z // 2 != z)
            def _():
                gsend(k).wait_send()

        for e in (0, 1):
            dest = lax.rem(2 * z + e, NZ)

            @pl.when(dest != z)
            def _():
                ref = cot_ref.at[:, pl.ds(e * q, q)]
                remote(ref, ref, cs.at[e], cr.at[0], tensor=dest).wait_send()

    all_of(condc_ref, a_s, a_r).wait_send()
    all_of(stc_ref, ts, tr).wait_send()
    ag_finish(1, stbuf, own_st)
    rs_finish(1)
    xy_finish(0, hid_ref)
    xy_finish(1, gp_ref)
    all_of(zbuf, zs, zrv).wait_send()
    all_of(pbuf, ps, prv).wait_send()
    save_pgrad.wait()
    save_lgrad.wait()
    save_gin.wait()
    with jax.named_scope("swap"):
        swap.wait_recv()
    stat_ref[0] = other[0, 0] + other[1, 0]
    stat_ref[1] = other[0, 1]
    swap.wait_send()


def token_side(x, cot, lift_w, proj_w, lmask, pmask, perm):
    tok, w = x.shape
    hw = lift_w.shape[0]
    feat = 2 * hw
    q = w // 2
    dma = pltpu.SemaphoreType.DMA
    vm = pl.BlockSpec(memory_space=pltpu.VMEM)
    sm = pl.BlockSpec(memory_space=pltpu.SMEM)
    hbm = pl.BlockSpec(memory_space=pl.ANY)
    n = NR * NR
    return pl.pallas_call(
        token_kernel,
        out_shape=(
            jax.ShapeDtypeStruct((tok, w), F32),
            jax.ShapeDtypeStruct((2, 8, BLK), F32),
            jax.ShapeDtypeStruct((BLK, w), F32),
            jax.ShapeDtypeStruct((q, w), F32),
        ),
        in_specs=[vm, vm, hbm, hbm, sm, sm, vm],
        out_specs=(hbm, vm, hbm, hbm),
        scratch_shapes=[
            pltpu.VMEM((NZ, tok, w), BF16),
            pltpu.VMEM((feat, hw), BF16),
            pltpu.VMEM((feat, 2 * w), BF16),
            pltpu.VMEM((hw, w), BF16),
            pltpu.VMEM((feat, w), BF16),
            pltpu.VMEM((tok, hw), BF16),
            pltpu.VMEM((tok, w), F32),
            pltpu.VMEM((tok, w), F32),
            pltpu.VMEM((tok, w), F32),
            pltpu.VMEM((NZ, tok, w), BF16),
            pltpu.VMEM((2, 2, 4, tok, w), BF16),
            pltpu.VMEM((2, 2, 4, tok, w), BF16),
            pltpu.VMEM((tok, w), BF16),
            pltpu.VMEM((tok, w), BF16),
            pltpu.VMEM((tok, w), BF16),
            pltpu.VMEM((tok, w), BF16),
            pltpu.VMEM((n, tok, BLK), BF16),
            pltpu.VMEM((n, tok, q), BF16),
            pltpu.VMEM((NR, NR, tok, w), BF16),
            pltpu.VMEM((NR, NR, tok, w), BF16),
            pltpu.VMEM((2, 8, BLK), F32),
            pltpu.VMEM((NZ, 2, 8, BLK), F32),
            pltpu.VMEM((2, 8, BLK), F32),
            pltpu.VMEM((n, 2, 8, BLK), F32),
            pltpu.VMEM((2, 2, 8, BLK), F32),
            pltpu.VMEM((tok, w), F32),
            pltpu.VMEM((BLK, w), F32),
            pltpu.VMEM((q, w), F32),
            dma((2,)),
            dma((3,)),
            dma((2, 4, NQ)),
            dma((2, 4, NQ)),
            dma((2, 4, NQ)),
            dma((2, 4, NQ)),
            dma((2,)),
            dma((2,)),
            dma((2,)),
            dma((2,)),
            dma,
            dma,
            dma,
            dma,
            dma,
            dma,
            dma((2, 2, 2, 2, 2)),
            dma((2, 2, 2, 2, 2)),
            dma,
            dma,
            dma,
            dma,
            dma,
            dma,
        ],
        compiler_params=pltpu.CompilerParams(
            collective_id=0, has_side_effects=True, vmem_limit_bytes=64 * 1024 * 1024 - 64 * 1024
        ),
        name="token_side",
    )(x, cot, lift_w, proj_w, lmask, pmask, perm)


def adam_kernel(
    lmask_ref,
    pmask_ref,
    stat_ref,
    lgrad_hbm,
    lmom_hbm,
    lsq_hbm,
    pgrad_hbm,
    pmom_hbm,
    psq_hbm,
    gin_hbm,
    lfirst_out,
    lsecond_out,
    lupdate_out,
    pfirst_out,
    psecond_out,
    pupdate_out,
    gin_out,
    log_ref,
    gin,
    grads,
    moms,
    sqs,
    news,
    in_s,
    out_s,
    gin_s,
    *,
    entries,
):
    me = lax.axis_index("dp_0") * NR + lax.axis_index("dp_1")
    n, rows, w = grads.shape
    blocks = []
    for b in range(n):
        r = pl.ds((b - 1) * rows, rows)
        if b == 0:
            ins = [lgrad_hbm, lmom_hbm.at[0], lsq_hbm.at[0]]
            outs = [lfirst_out.at[0], lsecond_out.at[0], lupdate_out.at[0]]
        else:
            ins = [pgrad_hbm.at[r], pmom_hbm.at[0, r], psq_hbm.at[0, r]]
            outs = [pfirst_out.at[0, r], psecond_out.at[0, r], pupdate_out.at[0, r]]
        loads = [
            pltpu.make_async_copy(ref, buf.at[b], in_s.at[b, k])
            for k, (ref, buf) in enumerate(zip(ins, (grads, moms, sqs)))
        ]
        saves = [pltpu.make_async_copy(news.at[b, k], ref, out_s.at[b, k]) for k, ref in enumerate(outs)]
        blocks.append((loads, saves))
    for loads, _ in blocks:
        for c in loads:
            c.start()
    gin_load = pltpu.make_async_copy(gin_hbm, gin, gin_s.at[0])
    gin_save = pltpu.make_async_copy(gin, gin_out.at[0], gin_s.at[1])
    gin_load.start()
    total = jnp.sum(stat_ref[0], keepdims=True)
    factor = jnp.minimum(1.0, CLIP / (jnp.sqrt(total) + 1e-06))
    log_ref[0] = jnp.sum(stat_ref[1]) * (1.0 / entries)
    bias_one = 1.0 - beta_one**ADAM_STEP
    bias_two = 1.0 - beta_two**ADAM_STEP
    for b, (loads, saves) in enumerate(blocks):
        for c in loads:
            c.wait()
        for c in range(w // BLK):
            cc = pl.ds(c * BLK, BLK)
            keep = (lmask_ref[c, me] if b == 0 else pmask_ref[c, me * (n - 1) + b - 1]) > 0
            moment = moms[b, :, cc]
            square = sqs[b, :, cc]
            scaled = grads[b, :, cc] * factor
            first = jnp.where(keep, beta_one * moment + (1.0 - beta_one) * scaled, moment)
            second = jnp.where(keep, beta_two * square + (1.0 - beta_two) * scaled * scaled, square)
            update = (first * (1.0 / bias_one)) / (jnp.sqrt(second * (1.0 / bias_two)) + adam_eps)
            news[b, 0, :, cc] = first
            news[b, 1, :, cc] = second
            news[b, 2, :, cc] = jnp.where(keep, update, 0.0)
        for c in saves:
            c.start()
    gin_load.wait()
    gin_save.start()
    gin_save.wait()
    for _, saves in blocks:
        for c in saves:
            c.wait()


def adam(entries, lmask, pmask, stat, lgrad, lmom, lsq, pgrad, pmom, psq, gin):
    dma = pltpu.SemaphoreType.DMA
    vm = pl.BlockSpec(memory_space=pltpu.VMEM)
    smem = pl.BlockSpec(memory_space=pltpu.SMEM)
    hbm = pl.BlockSpec(memory_space=pl.ANY)
    rows, w = lgrad.shape
    n = 1 + pgrad.shape[0] // rows
    like = jax.ShapeDtypeStruct
    return pl.pallas_call(
        functools.partial(adam_kernel, entries=entries),
        out_shape=(like(lmom.shape, F32),) * 3
        + (like(pmom.shape, F32),) * 3
        + (like((1,) + gin.shape, F32), like((1,), F32)),
        in_specs=[smem, smem, vm] + [hbm] * 7,
        out_specs=(hbm,) * 7 + (smem,),
        scratch_shapes=[
            pltpu.VMEM(gin.shape, F32),
            pltpu.VMEM((n, rows, w), F32),
            pltpu.VMEM((n, rows, w), F32),
            pltpu.VMEM((n, rows, w), F32),
            pltpu.VMEM((n, 3, rows, w), F32),
            dma((n, 3)),
            dma((n, 3)),
            dma((2,)),
        ],
        name="adam",
    )(lmask, pmask, stat, lgrad, lmom, lsq, pgrad, pmom, psq, gin)


def per_device(
    section_input,
    out_cotangent,
    lift_weight,
    proj_weight,
    lift_mask,
    proj_mask,
    channel_perm,
    lift_moment,
    lift_square,
    proj_moment,
    proj_square,
):
    lmask, pmask = lift_mask[0].T, proj_mask[0].T
    gin, stat, lift_grad, proj_grad = token_side(
        section_input[0], out_cotangent, lift_weight[0], proj_weight[0], lmask, pmask, channel_perm
    )
    tokens = NR * NR * gin.shape[0]
    *stepped, input_grad, log_det = adam(
        tokens * lift_weight.shape[1],
        lmask,
        pmask,
        stat,
        lift_grad,
        lift_moment,
        lift_square,
        proj_grad,
        proj_moment,
        proj_square,
        gin,
    )
    return (input_grad, log_det) + tuple(stepped)


def solution(mesh):
    finer = Mesh(
        mesh.devices.reshape(NR, NR, mesh.shape["tensor"], mesh.shape["layers"]),
        ("dp_0", "dp_1", "tensor", "layers"),
    )
    tiled = P("layers", DP, "tensor")
    weight = P("layers", None, "tensor")
    return jax.shard_map(
        per_device,
        mesh=finer,
        in_specs=(tiled, P(DP, "tensor")) + (weight,) * 4 + (P("layers", None),) + (tiled,) * 4,
        out_specs=(tiled, P("layers")) + (tiled,) * 6,
        check_vma=False,
    )
```

time: 166 us -> 125 us (0.75)
  Pallas kernels: 143 us -> 124 us
  other arithmetic: 6.12 us -> 0 us
  matrix products: 6 us -> 0 us
  local copies, waits for them, and re-layouts: 5.17 us -> 0 us
  between operations: 5.22 us -> 0.8 us
    pallas_call x1, Pallas kernels: 45.6 us -> 4.38 us  [adam(): pl.pallas_call(functools.partial(adam_kernel, entries=entries), out_shape...]
    pallas_call x1, Pallas kernels: 97.8 us -> 120 us  [token_side(): pl.pallas_call(token_kernel, out_shape=(jax.ShapeDtypeStruct((tok, w), F3...]
    dot_general x2 -> x0, matrix products: 6 us -> none  [tn(): lax.dot_general(a, b, (((0,), (0,)), ((), ())), preferred_element_type=F32)]
    squeeze x2 -> x0, local copies, waits for them, and re-layouts: 2.72 us -> none  [the longest x1 1.37 us: per_device(): proj_mask[0]]
    broadcast_in_dim x2 -> x0, other arithmetic: 2.47 us -> none  [adam_step(): return (new_first[None], new_second[None], update[None])]
where the time goes in v2:
time: 125 us
  Pallas kernels  124 us (99%)
    pallas_call x1, Pallas kernels, token_side(): pl.pallas_call(token_kernel, out_shape=(jax.ShapeDtypeStruct((tok, w), F3...  120 us
    pallas_call x1, Pallas kernels, adam(): pl.pallas_call(functools.partial(adam_kernel, entries=entries), out_shape...  4.38 us

profile of v2, /device:TPU:1, one launch (start us, length us, event | category | flops | bytes accessed | tf_op | source)
XLA Modules:
  0.0 124.9 jit_solution(16177300584138867381)
XLA Ops:
  0.6 119.7 %token_side.1 = (f32[128,512]{1,0:T(8,128)}, f32[2,8,128]{2,1,0:T(8,128)}, f32[128,512]{1,0:T(8,128)}, f32[256,512]{1,0:T(8,128)}) custom-call(bf16[128,512]{1,0:T(8,128)(2,1)} %bitcast.11, bf16[128,512]{1,0:T(8,128)(2,1)} %cot_ref.1, bf16[2048,512]{1,0:T(8,128)(2,1)} %bitcast.10, bf16[4096,512]{1,0:T(8,128)(2,1)} %bitcast.9, s32[4,16]{1,0:T(4,128)} %bitcast.12, ...), custom_call_target="tpu_custom_call" | custom-call | tf_op jit(solution)/shard_map/token_side/pallas_call | solution.py:725
  120.3 4.4 %adam.1 = (f32[1,128,512]{2,1,0:T(8,128)}, f32[1,128,512]{2,1,0:T(8,128)}, f32[1,128,512]{2,1,0:T(8,128)}, f32[1,256,512]{2,1,0:T(8,128)}, f32[1,256,512]{2,1,0:...) custom-call(s32[4,16]{1,0:T(4,128)} %bitcast.13, s32[4,32]{1,0:T(4,128)} %bitcast.15, ...), custom_call_target="tpu_custom_call" | custom-call | tf_op jit(solution)/shard_map/adam/pallas_call | solution.py:887

commit v3 on v2

--- a/solution.py
+++ b/solution.py
@@ -167,12 +167,12 @@
     def ag_copy(p, buf, own, s, d, h):
         origin = zr(-s) if d == 0 else zr(s)
         src = own.at[rows(h)] if s == 0 else buf.at[origin, rows(h)]
-        return remote(src, buf.at[origin, rows(h)], ag_s.at[d, s, h], ag_r.at[d, s, h], tensor=zside[d])
+        return remote(src, buf.at[origin, rows(h)], ag_s, ag_r.at[d, s, h], tensor=zside[d])
 
     def ag_wait(p, buf, s, d, h):
         origin = zr(-1 - s) if d == 0 else zr(1 + s)
         ref = buf.at[origin, rows(h)]
-        remote(ref, ref, ag_s.at[d, s, h], ag_r.at[d, s, h], tensor=zside[d]).wait_recv()
+        remote(ref, ref, ag_s, ag_r.at[d, s, h], tensor=zside[d]).wait_recv()
 
     def ag_start(p, buf, own):
         for k in range(NQ):
@@ -189,18 +189,15 @@
                         ag_copy(p, buf, own, s + 1, d, h).start()
         return [zr(-1 - s), zr(1 + s)] if s < 3 else [zr(4)]
 
-    def ag_finish(p, buf, own):
-        for d in (0, 1):
-            for s in range(4):
-                for h in range(NQ):
-                    if both_ways(d, s, h):
-                        ag_copy(p, buf, own, s, d, h).wait_send()
+    def ring_sent(ssem, rsem):
+        ref = xbuf.at[pl.ds(0, NZ - 1)]
+        remote(ref, ref, ssem, rsem.at[0, 0, 0], tensor=zside[0]).wait_send()
 
     def rs_copy(p, s, d, h):
         return remote(
             sbuf.at[p, d, s, rows(h)],
             rbuf.at[p, d, s, rows(h)],
-            rs_s.at[d, s, h],
+            rs_s,
             rs_r.at[d, s, h],
             tensor=zside[d],
         )
@@ -244,13 +241,6 @@
 
         return end
 
-    def rs_finish(p):
-        for d in (0, 1):
-            for s in range(4):
-                for h in range(NQ):
-                    if s > 0 or far(d, h):
-                        rs_copy(p, s, d, h).wait_send()
-
     def along(axis, i):
         if axis == "dp_1":
             return {"dp_1": lax.rem(x + NR + i, NR)}
@@ -271,38 +261,35 @@
     def xy_copy(p, buf, stage, h, t, d):
         axis = ("dp_1", "dp_0")[(h + stage) % 2]
         step = 1 if d == 0 else -1
-        src = slot(buf, stage, h, 0 if t == 0 else -step, xy_rows(h, t, d))
-        return remote(
-            src, src, xs.at[p, stage, h, t, d], xr.at[p, stage, h, t, d], **along(axis, step)
-        )
+        off = 0 if t == 0 else -step
+        rr = xy_rows(h, t, d)
+        if stage == 0 and t == 1:
+            step, off, rr = 2, 0, xy_rows(h, 0, 0)
+        src = slot(buf, stage, h, off, rr)
+        return remote(src, src, xs.at[p], xr.at[p, stage, h, t, d], **along(axis, step))
 
     def xy_wait(p, buf, stage, h, t, d):
-        axis = ("dp_1", "dp_0")[(h + stage) % 2]
         step = 1 if d == 0 else -1
-        ref = slot(buf, stage, h, -step if t == 0 else -2 * step, xy_rows(h, t, d))
-        remote(
-            ref, ref, xs.at[p, stage, h, t, d], xr.at[p, stage, h, t, d], **along(axis, step)
-        ).wait_recv()
+        off = -step if t == 0 else -2 * step
+        rr = xy_rows(h, 0 if stage == 0 else t, d)
+        ref = slot(buf, stage, h, off, rr)
+        remote(ref, ref, xs.at[p], xr.at[p, stage, h, t, d], tensor=zside[0]).wait_recv()
+
+    def xy_each(stage, t, act_on):
+        for h in (0, 1):
+            for d in (0,) if stage == 0 and t == 1 else (0, 1):
+                act_on(stage, h, t, d)
 
     def xy_tick(p, buf, k):
-        stage, t = k // 2, k % 2
         with jax.named_scope(f"xy{p}{k}"):
-            if k:
-                ps_, pt = (k - 1) // 2, (k - 1) % 2
-                for h in (0, 1):
-                    for d in (0, 1):
-                        xy_wait(p, buf, ps_, h, pt, d)
-            if k < 4:
-                for h in (0, 1):
-                    for d in (0, 1):
-                        xy_copy(p, buf, stage, h, t, d).start()
-
-    def xy_finish(p, buf):
-        for stage in (0, 1):
-            for h in (0, 1):
-                for t in (0, 1):
-                    for d in (0, 1):
-                        xy_copy(p, buf, stage, h, t, d).wait_send()
+            for stage, t in ((), ((0, 0), (0, 1)), ((1, 0),), ((1, 1),))[k]:
+                xy_each(stage, t, lambda *a: xy_wait(p, buf, *a))
+            for stage, t in (((0, 0), (0, 1)), ((1, 0),), ((1, 1),), ())[k]:
+                xy_each(stage, t, lambda *a: xy_copy(p, buf, *a).start())
+
+    def xy_finish(p):
+        ref = m.at[pl.ds(0, (NR * NR - 1) * tok // 2)]
+        remote(ref, ref, xs.at[p], xr.at[p, 0, 0, 0, 0], tensor=zside[0]).wait_send()
 
     def mask_lift(i, _):
         r = pl.ds(al(i * BLK, BLK), BLK)
@@ -396,7 +383,7 @@
         for origin in came:
             pre[...] += times(origin)
 
-    ag_finish(0, xbuf, x_ref)
+    ring_sent(ag_s, ag_r)
 
     squash = jax.nn.sigmoid(pre[...])
     slope[...] = squash * (1.0 + pre[...] * (1.0 - squash))
@@ -422,7 +409,7 @@
 
     with jax.named_scope("rs_shared"):
         shared = rs(0, shared_part, shared_tick)()
-    rs_finish(0)
+    ring_sent(rs_s, rs_r)
     raw = shared[:, :q] + 2.0
     scale = jax.nn.sigmoid(raw)
     sm[:, pl.ds(0, q)] = scale
@@ -470,7 +457,6 @@
     @pl.when(core == 0)
     def _():
         permute_tokens(0, hw // q)
-        xy_tick(0, hid_ref, 2)
         with jax.named_scope("handwait"):
             remote(gbuf, c0buf, hs, hr, layers=1 - core).wait_recv()
         cown[...] = c0buf[...]
@@ -534,11 +520,11 @@
             def _():
                 permute_tokens(5, hw // q)
 
-        if s == 1:
+        if s == 0:
 
             @pl.when(core == 0)
             def _():
-                xy_tick(0, hid_ref, 3)
+                xy_tick(0, hid_ref, 2)
 
         if s == 2:
 
@@ -560,9 +546,11 @@
         return jnp.concatenate([nt(lhs, m[in_rows(d, 0), :]), nt(lhs, m[in_rows(d, 1), :])], axis=1)
 
     def in_tick(s):
-        @pl.when(core == 0)
-        def _():
-            xy_tick(1, gp_ref, s)
+        if s < 3:
+
+            @pl.when(core == 0)
+            def _():
+                xy_tick(1, gp_ref, s)
 
         if s == 1:
             for i in (-3, 3, 4):
@@ -597,8 +585,6 @@
         xy_tick(1, gp_ref, 1)
         xy_tick(0, hid_ref, 3)
         xy_tick(1, gp_ref, 2)
-        xy_tick(0, hid_ref, 4)
-        xy_tick(1, gp_ref, 3)
 
     tokens = NR * NR * tok
 
@@ -611,7 +597,7 @@
 
     @pl.when(core == 0)
     def _():
-        xy_tick(0, hid_ref, 4)
+        xy_tick(0, hid_ref, 3)
 
     with jax.named_scope("stcome"):
         all_of(stc_ref, ts, tr).wait_recv()
@@ -624,7 +610,7 @@
     vec[0] = squares(pgrad_ref[...])
     with jax.named_scope("condwait"):
         all_of(condc_ref, a_s, a_r).wait_recv()
-    xy_tick(1, gp_ref, 4)
+    xy_tick(1, gp_ref, 3)
     with jax.named_scope("lgrad"):
         lgrad_ref[...] = tn(condc_ref[...].reshape(tokens, BLK), gp_ref[...].reshape(tokens, w))
     for c in range(w // BLK):
@@ -671,40 +657,41 @@
     for o in range(1, NR * NR):
         pcopy(o).start()
     pbuf[me] = mid[...]
+    @pl.when(core == 1)
+    def _():
+        remote(cown, c0buf, hs, hr, layers=1 - core).wait_send()
+        for k in (0, 1):
+
+            @pl.when(4 * k + z // 2 != z)
+            def _():
+                gsend(k).wait_send()
+
+        for e in (0, 1):
+            dest = lax.rem(2 * z + e, NZ)
+
+            @pl.when(dest != z)
+            def _():
+                ref = cot_ref.at[:, pl.ds(e * q, q)]
+                remote(ref, ref, cs.at[e], cr.at[0], tensor=dest).wait_send()
+
+    all_of(condc_ref, a_s, a_r).wait_send()
+    all_of(stc_ref, ts, tr).wait_send()
+    ring_sent(ag_s, ag_r)
+    ring_sent(rs_s, rs_r)
+    xy_finish(0)
+    xy_finish(1)
+    save_pgrad.wait()
+    save_lgrad.wait()
+    save_gin.wait()
+    all_of(zbuf, zs, zrv).wait_send()
+
     with jax.named_scope("psum"):
         all_of(pbuf, ps, prv).wait_recv()
     other[0] = jnp.sum(pbuf[...], axis=0)
     swap = remote(other.at[0], other.at[1], ls, lr, layers=1 - core)
     swap.start()
 
-    @pl.when(core == 1)
-    def _():
-        remote(cown, c0buf, hs, hr, layers=1 - core).wait_send()
-        for k in (0, 1):
-
-            @pl.when(4 * k + z // 2 != z)
-            def _():
-                gsend(k).wait_send()
-
-        for e in (0, 1):
-            dest = lax.rem(2 * z + e, NZ)
-
-            @pl.when(dest != z)
-            def _():
-                ref = cot_ref.at[:, pl.ds(e * q, q)]
-                remote(ref, ref, cs.at[e], cr.at[0], tensor=dest).wait_send()
-
-    all_of(condc_ref, a_s, a_r).wait_send()
-    all_of(stc_ref, ts, tr).wait_send()
-    ag_finish(1, stbuf, own_st)
-    rs_finish(1)
-    xy_finish(0, hid_ref)
-    xy_finish(1, gp_ref)
-    all_of(zbuf, zs, zrv).wait_send()
     all_of(pbuf, ps, prv).wait_send()
-    save_pgrad.wait()
-    save_lgrad.wait()
-    save_gin.wait()
     with jax.named_scope("swap"):
         swap.wait_recv()
     stat_ref[0] = other[0, 0] + other[1, 0]
@@ -763,9 +750,9 @@
             pltpu.VMEM((q, w), F32),
             dma((2,)),
             dma((3,)),
+            dma,
             dma((2, 4, NQ)),
-            dma((2, 4, NQ)),
-            dma((2, 4, NQ)),
+            dma,
             dma((2, 4, NQ)),
             dma((2,)),
             dma((2,)),
@@ -777,7 +764,7 @@
             dma,
             dma,
             dma,
-            dma((2, 2, 2, 2, 2)),
+            dma((2,)),
             dma((2, 2, 2, 2, 2)),
             dma,
             dma,

time: 125 us -> 120 us (0.960)
  Pallas kernels: 124 us -> 119 us
    pallas_call x1, Pallas kernels: 120 us -> 115 us  [token_side(): pl.pallas_call(token_kernel, out_shape=(jax.ShapeDtypeStruct((tok, w), F3...]
where the time goes in v3:
time: 120 us
  Pallas kernels  119 us (99%)
    pallas_call x1, Pallas kernels, token_side(): pl.pallas_call(token_kernel, out_shape=(jax.ShapeDtypeStruct((tok, w), F3...  115 us
    pallas_call x1, Pallas kernels, adam(): pl.pallas_call(functools.partial(adam_kernel, entries=entries), out_shape...  4.38 us

profile of v3, /device:TPU:1, one launch (start us, length us, event | category | flops | bytes accessed | tf_op | source)
XLA Modules:
  0.0 119.8 jit_solution(4387949746348682078)
XLA Ops:
  0.6 114.6 %token_side.1 = (f32[128,512]{1,0:T(8,128)}, f32[2,8,128]{2,1,0:T(8,128)}, f32[128,512]{1,0:T(8,128)}, f32[256,512]{1,0:T(8,128)}) custom-call(bf16[128,512]{1,0:T(8,128)(2,1)} %bitcast.11, bf16[128,512]{1,0:T(8,128)(2,1)} %cot_ref.1, bf16[2048,512]{1,0:T(8,128)(2,1)} %bitcast.10, bf16[4096,512]{1,0:T(8,128)(2,1)} %bitcast.9, s32[4,16]{1,0:T(4,128)} %bitcast.12, ...), custom_call_target="tpu_custom_call" | custom-call | tf_op jit(solution)/shard_map/token_side/pallas_call | solution.py:712
  115.3 4.4 %adam.1 = (f32[1,128,512]{2,1,0:T(8,128)}, f32[1,128,512]{2,1,0:T(8,128)}, f32[1,128,512]{2,1,0:T(8,128)}, f32[1,256,512]{2,1,0:T(8,128)}, f32[1,256,512]{2,1,0:...) custom-call(s32[4,16]{1,0:T(4,128)} %bitcast.13, s32[4,32]{1,0:T(4,128)} %bitcast.15, ...), custom_call_target="tpu_custom_call" | custom-call | tf_op jit(solution)/shard_map/adam/pallas_call | solution.py:874

commit v4 on v3

--- a/solution.py
+++ b/solution.py
@@ -351,10 +351,10 @@
     spread(zr(-1))
     with jax.named_scope("barrier"):
         pl.semaphore_wait(bar, NZ - 1 + NR * NR - 1 + 1)
-    ag_start(0, xbuf, x_ref)
 
     @pl.when(core == 1)
     def _():
+        ag_start(0, xbuf, x_ref)
         for e in (0, 1):
             dest = lax.rem(2 * z + e, NZ)
             piece = cot_ref.at[:, pl.ds(e * q, q)]
@@ -375,6 +375,11 @@
     load_proj.wait()
     with jax.named_scope("mask_proj"):
         lax.fori_loop(0, 2 * hw // BLK, mask_proj, 0)
+
+    @pl.when(core == 0)
+    def _():
+        ag_start(0, xbuf, x_ref)
+
     for s in range(4):
         with jax.named_scope(f"agx{s}"):
             came = ag_step(0, xbuf, x_ref, s)
@@ -546,13 +551,12 @@
         return jnp.concatenate([nt(lhs, m[in_rows(d, 0), :]), nt(lhs, m[in_rows(d, 1), :])], axis=1)
 
     def in_tick(s):
-        if s < 3:
+        if s == 1:
 
             @pl.when(core == 0)
             def _():
-                xy_tick(1, gp_ref, s)
-
-        if s == 1:
+                xy_tick(1, gp_ref, 1)
+
             for i in (-3, 3, 4):
                 st_send(zr(i))
 
@@ -598,6 +602,7 @@
     @pl.when(core == 0)
     def _():
         xy_tick(0, hid_ref, 3)
+        xy_tick(1, gp_ref, 2)
 
     with jax.named_scope("stcome"):
         all_of(stc_ref, ts, tr).wait_recv()

time: 120 us -> 120 us (level)
  no operation moved by 1% of the time
where the time goes in v4:
time: 120 us
  Pallas kernels  119 us (99%)
    pallas_call x1, Pallas kernels, token_side(): pl.pallas_call(token_kernel, out_shape=(jax.ShapeDtypeStruct((tok, w), F3...  115 us
    pallas_call x1, Pallas kernels, adam(): pl.pallas_call(functools.partial(adam_kernel, entries=entries), out_shape...  4.38 us

profile of v4, /device:TPU:1, one launch (start us, length us, event | category | flops | bytes accessed | tf_op | source)
XLA Modules:
  0.0 120.1 jit_solution(17991245491272055307)
XLA Ops:
  0.6 114.9 %token_side.1 = (f32[128,512]{1,0:T(8,128)}, f32[2,8,128]{2,1,0:T(8,128)}, f32[128,512]{1,0:T(8,128)}, f32[256,512]{1,0:T(8,128)}) custom-call(bf16[128,512]{1,0:T(8,128)(2,1)} %bitcast.11, bf16[128,512]{1,0:T(8,128)(2,1)} %cot_ref.1, bf16[2048,512]{1,0:T(8,128)(2,1)} %bitcast.10, bf16[4096,512]{1,0:T(8,128)(2,1)} %bitcast.9, s32[4,16]{1,0:T(4,128)} %bitcast.12, ...), custom_call_target="tpu_custom_call" | custom-call | tf_op jit(solution)/shard_map/token_side/pallas_call | solution.py:717
  115.5 4.4 %adam.1 = (f32[1,128,512]{2,1,0:T(8,128)}, f32[1,128,512]{2,1,0:T(8,128)}, f32[1,128,512]{2,1,0:T(8,128)}, f32[1,256,512]{2,1,0:T(8,128)}, f32[1,256,512]{2,1,0:...) custom-call(s32[4,16]{1,0:T(4,128)} %bitcast.13, s32[4,32]{1,0:T(4,128)} %bitcast.15, ...), custom_call_target="tpu_custom_call" | custom-call | tf_op jit(solution)/shard_map/adam/pallas_call | solution.py:879

commit v5 on v3

--- a/solution.py
+++ b/solution.py
@@ -546,11 +546,11 @@
         return jnp.concatenate([nt(lhs, m[in_rows(d, 0), :]), nt(lhs, m[in_rows(d, 1), :])], axis=1)
 
     def in_tick(s):
-        if s < 3:
+        if s != 2:
 
             @pl.when(core == 0)
             def _():
-                xy_tick(1, gp_ref, s)
+                xy_tick(1, gp_ref, (s + 1) // 2)
 
         if s == 1:
             for i in (-3, 3, 4):
@@ -812,12 +812,13 @@
 ):
     me = lax.axis_index("dp_0") * NR + lax.axis_index("dp_1")
     n, rows, w = grads.shape
+    per = BLK // rows
     blocks = []
     for b in range(n):
-        r = pl.ds((b - 1) * rows, rows)
-        if b == 0:
-            ins = [lgrad_hbm, lmom_hbm.at[0], lsq_hbm.at[0]]
-            outs = [lfirst_out.at[0], lsecond_out.at[0], lupdate_out.at[0]]
+        r = pl.ds((b if b < per else b - per) * rows, rows)
+        if b < per:
+            ins = [lgrad_hbm.at[r], lmom_hbm.at[0, r], lsq_hbm.at[0, r]]
+            outs = [lfirst_out.at[0, r], lsecond_out.at[0, r], lupdate_out.at[0, r]]
         else:
             ins = [pgrad_hbm.at[r], pmom_hbm.at[0, r], psq_hbm.at[0, r]]
             outs = [pfirst_out.at[0, r], psecond_out.at[0, r], pupdate_out.at[0, r]]
@@ -843,7 +844,7 @@
             c.wait()
         for c in range(w // BLK):
             cc = pl.ds(c * BLK, BLK)
-            keep = (lmask_ref[c, me] if b == 0 else pmask_ref[c, me * (n - 1) + b - 1]) > 0
+            keep = (lmask_ref[c, me] if b < per else pmask_ref[c, me * (n // per - 1) + b // per - 1]) > 0
             moment = moms[b, :, cc]
             square = sqs[b, :, cc]
             scaled = grads[b, :, cc] * factor
@@ -868,8 +869,8 @@
     vm = pl.BlockSpec(memory_space=pltpu.VMEM)
     smem = pl.BlockSpec(memory_space=pltpu.SMEM)
     hbm = pl.BlockSpec(memory_space=pl.ANY)
-    rows, w = lgrad.shape
-    n = 1 + pgrad.shape[0] // rows
+    rows, w = BLK // 2, lgrad.shape[1]
+    n = (lgrad.shape[0] + pgrad.shape[0]) // rows
     like = jax.ShapeDtypeStruct
     return pl.pallas_call(
         functools.partial(adam_kernel, entries=entries),

time: 120 us -> 120 us (level)
  no operation moved by 1% of the time
where the time goes in v5:
time: 120 us
  Pallas kernels  119 us (99%)
    pallas_call x1, Pallas kernels, token_side(): pl.pallas_call(token_kernel, out_shape=(jax.ShapeDtypeStruct((tok, w), F3...  115 us
    pallas_call x1, Pallas kernels, adam(): pl.pallas_call(functools.partial(adam_kernel, entries=entries), out_shape...  4.41 us

profile of v5, /device:TPU:1, one launch (start us, length us, event | category | flops | bytes accessed | tf_op | source)
XLA Modules:
  0.0 119.8 jit_solution(3763132835833350820)
XLA Ops:
  0.6 114.6 %token_side.1 = (f32[128,512]{1,0:T(8,128)}, f32[2,8,128]{2,1,0:T(8,128)}, f32[128,512]{1,0:T(8,128)}, f32[256,512]{1,0:T(8,128)}) custom-call(bf16[128,512]{1,0:T(8,128)(2,1)} %bitcast.11, bf16[128,512]{1,0:T(8,128)(2,1)} %cot_ref.1, bf16[2048,512]{1,0:T(8,128)(2,1)} %bitcast.10, bf16[4096,512]{1,0:T(8,128)(2,1)} %bitcast.9, s32[4,16]{1,0:T(4,128)} %bitcast.12, ...), custom_call_target="tpu_custom_call" | custom-call | tf_op jit(solution)/shard_map/token_side/pallas_call | solution.py:712
  115.3 4.4 %adam.1 = (f32[1,128,512]{2,1,0:T(8,128)}, f32[1,128,512]{2,1,0:T(8,128)}, f32[1,128,512]{2,1,0:T(8,128)}, f32[1,256,512]{2,1,0:T(8,128)}, f32[1,256,512]{2,1,0:...) custom-call(s32[4,16]{1,0:T(4,128)} %bitcast.13, s32[4,32]{1,0:T(4,128)} %bitcast.15, ...), custom_call_target="tpu_custom_call" | custom-call | tf_op jit(solution)/shard_map/adam/pallas_call | solution.py:875
